TPU v7x, 512 devices: a whole 4x8x8 slice. The times are simulated.
512 devices in a mesh: span: 16 (over z_hi, x), wall: 16 (over y, core), stream: 2 (over z_lo).
Axes of the slice: x: 4, y: 8, z: 8 (z_hi: 4, z_lo: 2; z = z_hi * 2 + z_lo), core: 2. Of those that a mesh axis runs over, the one named last changes fastest.
Arguments:
- fields: float32 [4, 16, 256, 2048], P(None, 'stream', 'wall', 'span'), may hold values from -67.5 to 67.5, as said below
Outputs:
- clark_model: float32 [3, 16, 256, 2048], P(None, 'stream', 'wall', 'span')
- similar_model: float32 [3, 16, 256, 2048], P(None, 'stream', 'wall', 'span')
- clark_corr: float32 [3, 256], P(None, 'wall')
- similar_corr: float32 [3, 256], P(None, 'wall')
Inputs may be any that keep to these rules, and one draw needn't show every extreme that they name: The fields are rough from cell to cell.
All inputs are finite; a program needn't handle non-finite values.
Results may differ from a plain program's by a relative error of at most 0.00024.
Values sent between devices are 32-bit elements; how exact they have to be, the bound alone decides.
A program may use at most 64 MiB of HBM per device.

v0:
```python
import math

import jax
import jax.numpy as jnp
from jax import lax
from jax.sharding import PartitionSpec as P

raw_taps = [math.exp(-((k - 8) ** 2) / 18.0) for k in range(17)]
filter_taps = [value / sum(raw_taps) for value in raw_taps]
clark_coef = 9.0
small_eps = 1e-06


def with_halo(cells, sides, width, closed):
    for axis, dim in sides:
        count = lax.axis_size(axis)
        ends = count if closed else count - 1
        head = lax.slice_in_dim(cells, 0, width, axis=dim)
        tail = lax.slice_in_dim(cells, cells.shape[dim] - width, cells.shape[dim], axis=dim)
        cells = jnp.concatenate(
            [
                lax.ppermute(tail, axis, [(i, (i + 1) % count) for i in range(ends)]),
                cells,
                lax.ppermute(head, axis, [((i + 1) % count, i) for i in range(ends)]),
            ],
            axis=dim,
        )
    return cells


def band_matrix(length):
    offset = (
        jnp.arange(length + 16, dtype=jnp.int32)[:, None]
        - jnp.arange(length, dtype=jnp.int32)[None, :]
    )
    matrix = jnp.zeros((length + 16, length), jnp.float32)
    for k in range(17):
        matrix = matrix + jnp.where(offset == k, filter_taps[k], 0.0).astype(jnp.float32)
    return matrix


def smooth(padded, direction, length):
    matrix = band_matrix(length)
    if direction == 3:
        return jnp.einsum("fswz,zk->fswk", padded, matrix, precision=lax.Precision.HIGHEST)
    if direction == 2:
        return jnp.einsum("fswz,wk->fskz", padded, matrix, precision=lax.Precision.HIGHEST)
    return jnp.einsum("fswz,sk->fkwz", padded, matrix, precision=lax.Precision.HIGHEST)


def with_products(quad):
    return jnp.concatenate([quad, quad[:3] * quad[3:4]], axis=0)


def filter_all(quad):
    stream_len, wall_len, span_len = (quad.shape[1], quad.shape[2], quad.shape[3])
    payload = with_products(quad)
    spanned = with_halo(payload, (("span", 3),), 8, True)
    extended = with_halo(spanned, (("wall", 2), ("stream", 1)), 8, False)
    kept = extended[:4]
    result = smooth(extended, 3, span_len)
    result = smooth(result, 2, wall_len)
    return (smooth(result, 1, stream_len), kept)


def clark_flux(means):
    padded = with_halo(means, (("span", 3),), 1, True)
    along_span = (padded[..., 2:] - padded[..., :-2]) * 0.5
    plane = with_halo(means, (("wall", 2), ("stream", 1)), 1, False)
    along_wall = (plane[:, 1:-1, 2:, :] - plane[:, 1:-1, :-2, :]) * 0.5
    along_stream = (plane[:, 2:, 1:-1, :] - plane[:, :-2, 1:-1, :]) * 0.5
    total = along_span[:3] * along_span[3:4] + along_wall[:3] * along_wall[3:4]
    total = total + along_stream[:3] * along_stream[3:4]
    return clark_coef * total


def shards(fields):
    first, unused_rim = filter_all(fields)
    means = first[:4]
    exact = first[4:] - means[:3] * means[3:4]
    second, mean_rim = filter_all(means)
    similar = second[4:] - second[:3] * second[3:4]
    clark = clark_flux(means)
    sums = (
        jnp.sum(exact * clark, axis=(1, 3)),
        jnp.sum(exact * similar, axis=(1, 3)),
        jnp.sum(exact * exact, axis=(1, 3)),
        jnp.sum(clark * clark, axis=(1, 3)),
        jnp.sum(similar * similar, axis=(1, 3)),
    )
    cross_c, cross_s, power_e, power_c, power_s = lax.psum(
        (sums[0], sums[1], sums[2], sums[3], sums[4]), ("span", "stream")
    )
    plane_cells = float(
        fields.shape[1] * fields.shape[3] * lax.axis_size("stream") * lax.axis_size("span")
    )
    cross_c = cross_c / plane_cells
    cross_s = cross_s / plane_cells
    power_e = power_e / plane_cells
    power_c = power_c / plane_cells
    power_s = power_s / plane_cells
    clark_corr = cross_c / jnp.sqrt((power_e + small_eps) * (power_c + small_eps))
    similar_corr = cross_s / jnp.sqrt((power_e + small_eps) * (power_s + small_eps))
    clark_model = clark / jnp.sqrt(power_c + small_eps)[:, None, :, None]
    similar_model = similar / jnp.sqrt(power_s + small_eps)[:, None, :, None]
    return (clark_model, similar_model, clark_corr, similar_corr)


def solution(mesh):
    return jax.shard_map(
        shards,
        mesh=mesh,
        in_specs=(P(None, "stream", "wall", "span"),),
        out_specs=(
            P(None, "stream", "wall", "span"),
            P(None, "stream", "wall", "span"),
            P(None, "wall"),
            P(None, "wall"),
        ),
        check_vma=False,
    )
```

profile of v0, /device:TPU:16, one launch (start us, length us, event | category | flops | bytes accessed | tf_op | source)
XLA Modules:
  0.0 371.7 jit_solution(2666519787292298506)
XLA Ops:
  3.7 13.1 %collective-permute-start.1 = (f32[7,8,16,8]{3,2,1,0:T(8,128)S(1)}, f32[7,8,16,8]{3,2,1,0:T(8,128)S(1)}, u32[]{:S(2)}, u32[]{:S(2)}) collective-permute-start(f32[7,8,16,8]{3,2,1,0:T(8,128)S(1)} %get-tuple-element.31), channel_id=1, source_target_pairs={{32,0},{64,32},{96,64},{128,96},{160,128},{192,160},{224,192},{256... | collective-permute-start | bytes 86024 | tf_op jit(solution)/shard_map/ppermute | solution.py:24
  16.9 1.9 collective-permute-start
  18.8 17.7 %collective-permute-done.1 = f32[7,8,16,8]{3,2,1,0:T(8,128)S(1)} collective-permute-done((f32[7,8,16,8]{3,2,1,0:T(8,128)S(1)}, f32[7,8,16,8]{3,2,1,0:T(8,128)S(1)}, u32[]{:S(2)}, u32[]{:S(2)}) %collective-permute-start.1) | collective-permute-done | bytes 28704 | tf_op jit(solution)/shard_map/ppermute | solution.py:24
  36.4 8.3 %collective-permute-done = f32[7,8,16,8]{3,2,1,0:T(8,128)S(1)} collective-permute-done((f32[7,8,16,8]{3,2,1,0:T(8,128)S(1)}, f32[7,8,16,8]{3,2,1,0:T(8,128)S(1)}, u32[]{:S(2)}, u32[]{:S(2)}) %collective-permute-start) | collective-permute-done | bytes 28704 | tf_op jit(solution)/shard_map/ppermute | solution.py:22
  46.3 1.9 collective-permute-start.3
  48.2 2.4 collective-permute-start.2
  50.6 3.6 collective-permute-done.3
  54.2 3.8 %collective-permute-done.2 = f32[7,8,8,144]{3,2,1,0:T(8,128)S(1)} collective-permute-done((f32[7,8,8,144]{3,2,1,0:T(8,128)S(1)}, f32[7,8,8,144]{3,2,1,0:T(8,128)S(1)}, u32[]{:S(2)}, u32[]{:S(2)}) %collective-permute-start.2) | collective-permute-done | bytes 258080 | tf_op jit(solution)/shard_map/ppermute | solution.py:22
  59.8 4.8 %collective-permute-start.4 = (f32[7,8,32,144]{3,2,1,0:T(8,128)S(1)}, f32[7,8,32,144]{3,2,1,0:T(8,128)S(1)}, u32[]{:S(2)}, u32[]{:S(2)}) collective-permute-start(f32[7,8,32,144]{3,2,1,0:T(8,128)S(1)} %pad_maximum_fusion.1), channel_id=1, source_target_pairs={{0,1},{2,3},{4,5},{6,7},{8,9},{10,11},{12,13},{14,15},{16,17},{18,... | collective-permute-start | bytes 3096584 | tf_op jit(solution)/shard_map/ppermute | solution.py:22
  64.5 36.9 %collective-permute-done.5 = f32[7,8,32,144]{3,2,1,0:T(8,128)S(1)} collective-permute-done((f32[7,8,32,144]{3,2,1,0:T(8,128)S(1)}, f32[7,8,32,144]{3,2,1,0:T(8,128)S(1)}, u32[]{:S(2)}, u32[]{:S(2)}) %collective-permute-start.5) | collective-permute-done | bytes 1032224 | tf_op jit(solution)/shard_map/ppermute | solution.py:24
  102.8 4.7 %fusion = f32[7,24,32,128]{3,2,1,0:T(8,128)S(1)} fusion(f32[7,8,32,144]{3,2,1,0:T(8,128)S(1)} %collective-permute-done.5, f32[7,8,8,144]{3,2,1,0:T(8,128)S(1)} %collective-permute-done.3, f32[7,8,16,8]{3,2,1,0:T(8,128)S(1)} %collective-permute-done.1, f32[3,8,16,128]{3,2,1,0:T(8,128)S(1)} %slice_multiply_fusion.5, f32[4,8,16,128]{3,2,1,0:T(8,128)S(1)} %copy-done, ...), kind=kOutput, calls=%fused_computation | convolution fusion | flops 1195444224 | bytes 5849088 | tf_op jit(solution)/shard_map/fswz,zk->fswk/dot_general | solution.py:45
  107.5 1.5 fusion.61
  110.5 1.9 collective-permute-start.13
  112.4 3.9 %collective-permute-start.12 = (f32[7,8,16,8]{3,1,2,0:T(8,128)S(1)}, f32[7,8,16,8]{3,1,2,0:T(8,128)S(1)}, u32[]{:S(2)}, u32[]{:S(2)}) collective-permute-start(f32[7,8,16,8]{3,1,2,0:T(8,128)S(1)} %get-tuple-element.28), channel_id=1, source_target_pairs={{0,32},{32,64},{64,96},{96,128},{128,160},{160,192},{192,224},{224... | collective-permute-start | bytes 86024 | tf_op jit(solution)/shard_map/ppermute | solution.py:22
  116.3 14.1 %collective-permute-done.13 = f32[7,8,16,8]{3,1,2,0:T(8,128)S(1)} collective-permute-done((f32[7,8,16,8]{3,1,2,0:T(8,128)S(1)}, f32[7,8,16,8]{3,1,2,0:T(8,128)S(1)}, u32[]{:S(2)}, u32[]{:S(2)}) %collective-permute-start.13) | collective-permute-done | bytes 28704 | tf_op jit(solution)/shard_map/ppermute | solution.py:24
  130.4 8.3 %collective-permute-done.12 = f32[7,8,16,8]{3,1,2,0:T(8,128)S(1)} collective-permute-done((f32[7,8,16,8]{3,1,2,0:T(8,128)S(1)}, f32[7,8,16,8]{3,1,2,0:T(8,128)S(1)}, u32[]{:S(2)}, u32[]{:S(2)}) %collective-permute-start.12) | collective-permute-done | bytes 28704 | tf_op jit(solution)/shard_map/ppermute | solution.py:22
  139.3 1.9 collective-permute-start.15
  141.2 2.4 collective-permute-start.14
  143.6 3.6 collective-permute-done.15
  147.2 3.8 %collective-permute-done.14 = f32[7,8,8,144]{3,1,2,0:T(8,128)S(1)} collective-permute-done((f32[7,8,8,144]{3,1,2,0:T(8,128)S(1)}, f32[7,8,8,144]{3,1,2,0:T(8,128)S(1)}, u32[]{:S(2)}, u32[]{:S(2)}) %collective-permute-start.14) | collective-permute-done | bytes 258080 | tf_op jit(solution)/shard_map/ppermute | solution.py:22
  152.7 4.8 %collective-permute-start.16 = (f32[7,8,32,144]{3,1,2,0:T(8,128)S(1)}, f32[7,8,32,144]{3,1,2,0:T(8,128)S(1)}, u32[]{:S(2)}, u32[]{:S(2)}) collective-permute-start(f32[7,8,32,144]{3,1,2,0:T(8,128)S(1)} %pad_maximum_fusion.2), channel_id=1, source_target_pairs={{0,1},{2,3},{4,5},{6,7},{8,9},{10,11},{12,13},{14,15},{16,17},{18,... | collective-permute-start | bytes 3096584 | tf_op jit(solution)/shard_map/ppermute | solution.py:22
  157.5 3.3 collective-permute-start.9
  160.8 2.5 collective-permute-start.8
  163.3 3.1 collective-permute-done.8
  169.2 1.9 collective-permute-start.7
  171.2 38.2 %collective-permute-done.7 = f32[4,8,16,1]{3,1,2,0:T(8,128)S(1)} collective-permute-done((f32[4,8,16,1]{3,1,2,0:T(8,128)S(1)}, f32[4,8,16,1]{3,1,2,0:T(8,128)S(1)}, u32[]{:S(2)}, u32[]{:S(2)}) %collective-permute-start.7) | collective-permute-done | bytes 2080 | tf_op jit(solution)/shard_map/ppermute | solution.py:22
  209.3 1.9 collective-permute-start.6
  211.2 8.4 %collective-permute-done.6 = f32[4,8,16,1]{3,1,2,0:T(8,128)S(1)} collective-permute-done((f32[4,8,16,1]{3,1,2,0:T(8,128)S(1)}, f32[4,8,16,1]{3,1,2,0:T(8,128)S(1)}, u32[]{:S(2)}, u32[]{:S(2)}) %collective-permute-start.6) | collective-permute-done | bytes 2080 | tf_op jit(solution)/shard_map/ppermute | solution.py:24
  220.1 2.6 pad_maximum_fusion
  222.7 5.8 %fusion.16 = f32[7,24,32,128]{3,2,1,0:T(8,128)S(1)} fusion(f32[7,24,32,144]{3,1,2,0:T(8,128)S(1)} %pad_maximum_fusion), kind=kOutput, calls=%fused_computation.17 | convolution fusion | flops 1190025216 | bytes 5849088 | tf_op jit(solution)/shard_map/fswz,zk->fswk/dot_general | solution.py:45
  228.5 1.5 fusion.59
  231.8 137.7 %all-reduce = (f32[3,16]{1,0:T(4,128)S(1)}, f32[3,16]{1,0:T(4,128)S(1)}, f32[3,16]{1,0:T(4,128)S(1)}, f32[3,16]{1,0:T(4,128)S(1)}, f32[3,16]{1,0:T(4,128)S(1)}) all-reduce(f32[3,16]{1,0:T(4,128)S(1)} %get-tuple-element.11, f32[3,16]{1,0:T(4,128)S(1)} %get-tuple-element.12, ...), channel_id=1, replica_groups=mesh['span'=16,'wall'=16,'stream'=2] {'span','stream'}, use_global_device_ids=true, to_apply=%region_1.2 | all-reduce | flops 240 | bytes 1920 | tf_op jit(solution)/shard_map/psum | solution.py:91
  (40 shorter events, 18.4 us)
Async XLA Ops:
  2.4 55.6 %copy-start = (f32[4,8,16,128]{3,2,1,0:T(8,128)S(1)}, f32[4,8,16,128]{3,2,1,0:T(8,128)}, u32[]{:S(2)}) copy-start(f32[4,8,16,128]{3,2,1,0:T(8,128)} %param.1) | copy-start | bytes 786436
  3.7 32.7 %collective-permute-start.1 = (f32[7,8,16,8]{3,2,1,0:T(8,128)S(1)}, f32[7,8,16,8]{3,2,1,0:T(8,128)S(1)}, u32[]{:S(2)}, u32[]{:S(2)}) collective-permute-start(f32[7,8,16,8]{3,2,1,0:T(8,128)S(1)} %get-tuple-element.31), channel_id=1, source_target_pairs={{32,0},{64,32},{96,64},{128,96},{160,128},{192,160},{224,192},{256... | collective-permute-start | bytes 86024 | tf_op jit(solution)/shard_map/ppermute | solution.py:24
  16.9 27.9 %collective-permute-start = (f32[7,8,16,8]{3,2,1,0:T(8,128)S(1)}, f32[7,8,16,8]{3,2,1,0:T(8,128)S(1)}, u32[]{:S(2)}, u32[]{:S(2)}) collective-permute-start(f32[7,8,16,8]{3,2,1,0:T(8,128)S(1)} %get-tuple-element.30), channel_id=1, source_target_pairs={{0,32},{32,64},{64,96},{96,128},{128,160},{160,192},{192,224},{224... | collective-permute-start | bytes 86024 | tf_op jit(solution)/shard_map/ppermute | solution.py:22
  46.3 7.9 %collective-permute-start.3 = (f32[7,8,8,144]{3,2,1,0:T(8,128)S(1)}, f32[7,8,8,144]{3,2,1,0:T(8,128)S(1)}, u32[]{:S(2)}, u32[]{:S(2)}) collective-permute-start(f32[7,8,8,144]{3,2,1,0:T(8,128)S(1)} %get-tuple-element.23), channel_id=1, source_target_pairs={{2,0},{4,2},{6,4},{8,6},{10,8},{12,10},{14,12},{16,14},{18,16},{20... | collective-permute-start | bytes 774152 | tf_op jit(solution)/shard_map/ppermute | solution.py:24
  48.2 9.8 %collective-permute-start.2 = (f32[7,8,8,144]{3,2,1,0:T(8,128)S(1)}, f32[7,8,8,144]{3,2,1,0:T(8,128)S(1)}, u32[]{:S(2)}, u32[]{:S(2)}) collective-permute-start(f32[7,8,8,144]{3,2,1,0:T(8,128)S(1)} %get-tuple-element.22), channel_id=1, source_target_pairs={{0,2},{2,4},{4,6},{6,8},{8,10},{10,12},{12,14},{14,16},{16,18},{18... | collective-permute-start | bytes 774152 | tf_op jit(solution)/shard_map/ppermute | solution.py:22
  58.5 43.0 %collective-permute-start.5 = (f32[7,8,32,144]{3,2,1,0:T(8,128)S(1)}, f32[7,8,32,144]{3,2,1,0:T(8,128)S(1)}, u32[]{:S(2)}, u32[]{:S(2)}) collective-permute-start(f32[7,8,32,144]{3,2,1,0:T(8,128)S(1)} %pad_maximum_fusion.1), channel_id=1, source_target_pairs={{1,0},{3,2},{5,4},{7,6},{9,8},{11,10},{13,12},{15,14},{17,16},{19,... | collective-permute-start | bytes 3096584 | tf_op jit(solution)/shard_map/ppermute | solution.py:24
  59.8 43.0 %collective-permute-start.4 = (f32[7,8,32,144]{3,2,1,0:T(8,128)S(1)}, f32[7,8,32,144]{3,2,1,0:T(8,128)S(1)}, u32[]{:S(2)}, u32[]{:S(2)}) collective-permute-start(f32[7,8,32,144]{3,2,1,0:T(8,128)S(1)} %pad_maximum_fusion.1), channel_id=1, source_target_pairs={{0,1},{2,3},{4,5},{6,7},{8,9},{10,11},{12,13},{14,15},{16,17},{18,... | collective-permute-start | bytes 3096584 | tf_op jit(solution)/shard_map/ppermute | solution.py:22
  110.5 20.0 %collective-permute-start.13 = (f32[7,8,16,8]{3,1,2,0:T(8,128)S(1)}, f32[7,8,16,8]{3,1,2,0:T(8,128)S(1)}, u32[]{:S(2)}, u32[]{:S(2)}) collective-permute-start(f32[7,8,16,8]{3,1,2,0:T(8,128)S(1)} %get-tuple-element.29), channel_id=1, source_target_pairs={{32,0},{64,32},{96,64},{128,96},{160,128},{192,160},{224,192},{256... | collective-permute-start | bytes 86024 | tf_op jit(solution)/shard_map/ppermute | solution.py:24
  112.4 26.4 %collective-permute-start.12 = (f32[7,8,16,8]{3,1,2,0:T(8,128)S(1)}, f32[7,8,16,8]{3,1,2,0:T(8,128)S(1)}, u32[]{:S(2)}, u32[]{:S(2)}) collective-permute-start(f32[7,8,16,8]{3,1,2,0:T(8,128)S(1)} %get-tuple-element.28), channel_id=1, source_target_pairs={{0,32},{32,64},{64,96},{96,128},{128,160},{160,192},{192,224},{224... | collective-permute-start | bytes 86024 | tf_op jit(solution)/shard_map/ppermute | solution.py:22
  139.3 7.9 %collective-permute-start.15 = (f32[7,8,8,144]{3,1,2,0:T(8,128)S(1)}, f32[7,8,8,144]{3,1,2,0:T(8,128)S(1)}, u32[]{:S(2)}, u32[]{:S(2)}) collective-permute-start(f32[7,8,8,144]{3,1,2,0:T(8,128)S(1)} %get-tuple-element.21), channel_id=1, source_target_pairs={{2,0},{4,2},{6,4},{8,6},{10,8},{12,10},{14,12},{16,14},{18,16},{20... | collective-permute-start | bytes 774152 | tf_op jit(solution)/shard_map/ppermute | solution.py:24
  141.2 9.8 %collective-permute-start.14 = (f32[7,8,8,144]{3,1,2,0:T(8,128)S(1)}, f32[7,8,8,144]{3,1,2,0:T(8,128)S(1)}, u32[]{:S(2)}, u32[]{:S(2)}) collective-permute-start(f32[7,8,8,144]{3,1,2,0:T(8,128)S(1)} %get-tuple-element.20), channel_id=1, source_target_pairs={{0,2},{2,4},{4,6},{6,8},{8,10},{10,12},{12,14},{14,16},{16,18},{18... | collective-permute-start | bytes 774152 | tf_op jit(solution)/shard_map/ppermute | solution.py:22
  151.4 68.6 %collective-permute-start.17 = (f32[7,8,32,144]{3,1,2,0:T(8,128)S(1)}, f32[7,8,32,144]{3,1,2,0:T(8,128)S(1)}, u32[]{:S(2)}, u32[]{:S(2)}) collective-permute-start(f32[7,8,32,144]{3,1,2,0:T(8,128)S(1)} %pad_maximum_fusion.2), channel_id=1, source_target_pairs={{1,0},{3,2},{5,4},{7,6},{9,8},{11,10},{13,12},{15,14},{17,16},{19,... | collective-permute-start | bytes 3096584 | tf_op jit(solution)/shard_map/ppermute | solution.py:24
  152.7 67.3 %collective-permute-start.16 = (f32[7,8,32,144]{3,1,2,0:T(8,128)S(1)}, f32[7,8,32,144]{3,1,2,0:T(8,128)S(1)}, u32[]{:S(2)}, u32[]{:S(2)}) collective-permute-start(f32[7,8,32,144]{3,1,2,0:T(8,128)S(1)} %pad_maximum_fusion.2), channel_id=1, source_target_pairs={{0,1},{2,3},{4,5},{6,7},{8,9},{10,11},{12,13},{14,15},{16,17},{18,... | collective-permute-start | bytes 3096584 | tf_op jit(solution)/shard_map/ppermute | solution.py:22
  157.5 5.8 %collective-permute-start.9 = (f32[4,8,1,128]{3,1,2,0:T(8,128)S(1)}, f32[4,8,1,128]{3,1,2,0:T(8,128)S(1)}, u32[]{:S(2)}, u32[]{:S(2)}) collective-permute-start(f32[4,8,1,128]{3,1,2,0:T(8,128)S(1)} %get-tuple-element.26), channel_id=1, source_target_pairs={{0,2},{2,4},{4,6},{6,8},{8,10},{10,12},{12,14},{14,16},{16,18},{18... | collective-permute-start | bytes 49160 | tf_op jit(solution)/shard_map/ppermute | solution.py:22
  160.8 5.6 %collective-permute-start.8 = (f32[4,8,1,128]{3,1,2,0:T(8,128)S(1)}, f32[4,8,1,128]{3,1,2,0:T(8,128)S(1)}, u32[]{:S(2)}, u32[]{:S(2)}) collective-permute-start(f32[4,8,1,128]{3,1,2,0:T(8,128)S(1)} %get-tuple-element.27), channel_id=1, source_target_pairs={{2,0},{4,2},{6,4},{8,6},{10,8},{12,10},{14,12},{16,14},{18,16},{20... | collective-permute-start | bytes 49160 | tf_op jit(solution)/shard_map/ppermute | solution.py:24
  166.5 53.2 %collective-permute-start.11 = (f32[4,1,18,128]{3,1,2,0:T(1,128)S(1)}, f32[4,1,18,128]{3,1,2,0:T(1,128)S(1)}, u32[]{:S(2)}, u32[]{:S(2)}) collective-permute-start(f32[4,1,18,128]{3,1,2,0:T(1,128)S(1)} %get-tuple-element.35), channel_id=1, source_target_pairs={{0,1},{2,3},{4,5},{6,7},{8,9},{10,11},{12,13},{14,15},{16,17},{18,... | collective-permute-start | bytes 110600 | tf_op jit(solution)/shard_map/ppermute | solution.py:22
  167.8 51.9 %collective-permute-start.10 = (f32[4,1,18,128]{3,1,2,0:T(1,128)S(1)}, f32[4,1,18,128]{3,1,2,0:T(1,128)S(1)}, u32[]{:S(2)}, u32[]{:S(2)}) collective-permute-start(f32[4,1,18,128]{3,1,2,0:T(1,128)S(1)} %get-tuple-element.34), channel_id=1, source_target_pairs={{1,0},{3,2},{5,4},{7,6},{9,8},{11,10},{13,12},{15,14},{17,16},{19,... | collective-permute-start | bytes 110600 | tf_op jit(solution)/shard_map/ppermute | solution.py:24
  169.2 40.1 %collective-permute-start.7 = (f32[4,8,16,1]{3,1,2,0:T(8,128)S(1)}, f32[4,8,16,1]{3,1,2,0:T(8,128)S(1)}, u32[]{:S(2)}, u32[]{:S(2)}) collective-permute-start(f32[4,8,16,1]{3,1,2,0:T(8,128)S(1)} %get-tuple-element.25), channel_id=1, source_target_pairs={{0,32},{32,64},{64,96},{96,128},{128,160},{160,192},{192,224},{224... | collective-permute-start | bytes 6152 | tf_op jit(solution)/shard_map/ppermute | solution.py:22
  209.3 10.3 %collective-permute-start.6 = (f32[4,8,16,1]{3,1,2,0:T(8,128)S(1)}, f32[4,8,16,1]{3,1,2,0:T(8,128)S(1)}, u32[]{:S(2)}, u32[]{:S(2)}) collective-permute-start(f32[4,8,16,1]{3,1,2,0:T(8,128)S(1)} %get-tuple-element.24), channel_id=1, source_target_pairs={{32,0},{64,32},{96,64},{128,96},{160,128},{192,160},{224,192},{256... | collective-permute-start | bytes 6152 | tf_op jit(solution)/shard_map/ppermute | solution.py:24
where the time goes:
time: 372 us
  waiting for transfers between devices  151 us (41%)
  blocking collectives  138 us (37%)
  starting transfers between devices  53.8 us (14%)
  matrix products  15.9 us (4%)
  other arithmetic  9.48 us (3%)
    psum x1, blocking collectives, shards(): lax.psum((sums[0], sums[1], sums[2], sums[3], sums[4]), ('span', 'stream'))  138 us
    ppermute x9, waiting for transfers between devices, with_halo(): lax.ppermute(head, axis, [((i + 1) % count, i) for i in range(ends)])  87.4 us
    ppermute x9, waiting for transfers between devices, with_halo(): lax.ppermute(tail, axis, [(i, (i + 1) % count) for i in range(ends)])  63.8 us
    ppermute x9, starting transfers between devices, with_halo(): lax.ppermute(head, axis, [((i + 1) % count, i) for i in range(ends)])  27.1 us
    ppermute x9, starting transfers between devices, with_halo(): lax.ppermute(tail, axis, [(i, (i + 1) % count) for i in range(ends)])  26.7 us
    dot_general x2, matrix products, smooth(): jnp.einsum('fswz,zk->fswk', padded, matrix, precision=lax.Precision.HIGHEST)  10.5 us
  transfers between devices with their start and end apart: 18, of which 13 were waited for; matrix products, arithmetic and copies ran while one was open for 0% of the time, Pallas kernels for 0%

commit v1 on v0

v1 whole, which is shorter than its diff:
```python
import math

import jax
import jax.numpy as jnp
import ml_dtypes
import numpy as np
from jax import lax
from jax.experimental import pallas as pl
from jax.experimental.pallas import tpu as pltpu
from jax.sharding import PartitionSpec as P

raw_taps = [math.exp(-((k - 8) ** 2) / 18.0) for k in range(17)]
filter_taps = [value / sum(raw_taps) for value in raw_taps]
clark_coef = 9.0
small_eps = 1e-06

MESH = pl.DeviceIdType.MESH
BF = jnp.bfloat16
F32 = jnp.float32
ROW = 4
NQ = 5


def tap(out_at, in_at):
    offset = in_at - out_at + 8
    inside = (offset >= 0) & (offset <= 16)
    return np.where(inside, np.array(filter_taps)[np.clip(offset, 0, 16)], 0.0)


def split(matrix):
    full = matrix.astype(np.float32)
    hi = full.astype(ml_dtypes.bfloat16)
    lo = (full - hi.astype(np.float32)).astype(ml_dtypes.bfloat16)
    return hi, lo


def left_stack(matrix):
    hi, lo = split(matrix)
    return np.concatenate([hi, hi, lo], axis=1)


def right_stack(matrix):
    hi, lo = split(matrix)
    return np.concatenate([hi, hi, lo], axis=0)


def plane_matrices():
    s_out, w_out = np.meshgrid(np.arange(16), np.arange(16), indexing="ij")
    s_out, w_out = s_out.reshape(-1, 1), w_out.reshape(-1, 1)
    b, s, w = np.meshgrid(np.arange(2), np.arange(16), np.arange(16), indexing="ij")
    blocks = tap(s_out, s.reshape(1, -1)) * tap(w_out + 8, (b * 16 + w).reshape(1, -1))
    s, w = np.meshgrid(np.arange(16), np.arange(32), indexing="ij")
    rows = tap(s_out, s.reshape(1, -1)) * tap(w_out + 8, w.reshape(1, -1))
    own = np.stack([left_stack(rows[:128]), left_stack(rows[128:])])
    return left_stack(blocks), own


def span_matrices():
    lane = np.arange(128)
    group, inner = lane // 32, lane % 32
    place = np.where(inner < 16, inner - 16, inner + 112)
    kept = (inner >= 8) & (inner < 24)
    main = tap(lane[None, :], lane[:, None])
    result = []
    for f in range(4):
        from_rim = tap(lane[None, :], place[:, None]) * (group == f)[:, None]
        to_rim = tap(place[None, :], lane[:, None]) * ((group == f) & kept)[None, :]
        rim = tap(place[None, :], place[:, None]) * (group[:, None] == group[None, :])
        rim = rim * kept[None, :] * (1.0 if f == 0 else 0.0)
        result.append(right_stack(np.block([[main, to_rim], [from_rim, rim]])))
    return np.stack(result)


def hi_lo(values):
    hi = values.astype(BF)
    return hi, (values - hi.astype(F32)).astype(BF)


def rim_product(rims):
    lane = lax.broadcasted_iota(jnp.int32, rims.shape, 1)
    last = jnp.where(lane >= 96, rims, 0.0)
    last = last + pltpu.roll(last, 32, 1)
    last = last + pltpu.roll(last, 64, 1)
    return rims * last


def kernel(
    cells, fields, km_in, ko_in, w_in,
    clark_out, similar_out, cc_out, sc_out,
    x, edge, edge_in, km, ko, wm, yh, yl, m, mh, zs, st, st_a, st_t, st_b,
    loc, z_s, z_r, own_s, own_r, rel_s, rel_r, e_s, e_r, a_s, a_r, b_s, b_r,
):
    p, wl, s = lax.axis_index("span"), lax.axis_index("wall"), lax.axis_index("stream")
    np_, nw = lax.axis_size("span"), lax.axis_size("wall")
    nz = np_ // ROW
    xi, zi = p % ROW, p // ROW
    o = 1 - s
    mine = pl.multiple_of(s * 8, 8)
    theirs = pl.multiple_of(o * 8, 8)

    greet = [{"span": (p + 1) % np_}, {"span": (p + np_ - 1) % np_}]
    greet += [{"wall": (wl + 1) % nw}, {"wall": (wl + nw - 1) % nw}]
    row_mates = [
        {"span": zi * ROW + (xi + k // 2) % ROW, "stream": (s + k % 2) % 2}
        for k in range(1, 2 * ROW)
    ]
    col_mates = [{"span": ((zi + k) % nz) * ROW + xi} for k in range(1, nz)]
    greet += row_mates + col_mates

    local = [
        pltpu.make_async_copy(fields.at[f], x.at[f, 1, pl.ds(mine, 8)], loc.at[f])
        for f in range(4)
    ]
    local += [
        pltpu.make_async_copy(km_in, km, loc.at[4]),
        pltpu.make_async_copy(ko_in.at[s], ko, loc.at[5]),
        pltpu.make_async_copy(w_in, wm, loc.at[6]),
    ]
    for copy in local:
        copy.start()

    barrier = pltpu.get_barrier_semaphore()
    for device in greet:
        pl.semaphore_signal(barrier, inc=1, device_id=device, device_id_type=MESH)

    @pl.when(wl == 0)
    def _():
        x[:, 0] = jnp.zeros((NQ, 16, 16, 128), F32)

    @pl.when(wl == nw - 1)
    def _():
        x[:, 2] = jnp.zeros((NQ, 16, 16, 128), F32)

    for f in range(4):
        local[f].wait()

    lane = lax.broadcasted_iota(jnp.int32, (64, 128), 1)
    to_next = jnp.zeros((64, 128), F32)
    to_prev = jnp.zeros((64, 128), F32)
    for f in range(4):
        for half in range(2):
            part = x[f, 1, pl.ds(mine, 8), 8 * half : 8 * half + 8, :].reshape(64, 128)
            at = f * 32 + 16 * half
            here = (lane >= at) & (lane < at + 16)
            to_next = jnp.where(here, pltpu.roll(part, (at - 112) % 128, 1), to_next)
            at = f * 32 + 16 * (1 - half)
            here = (lane >= at) & (lane < at + 16)
            to_prev = jnp.where(here, pltpu.roll(part, at % 128, 1) if at else part, to_prev)
    edge[0] = to_next.reshape(8, 8, 128)
    edge[1] = to_prev.reshape(8, 8, 128)

    pl.semaphore_wait(barrier, len(greet))

    edges = [
        pltpu.make_async_remote_copy(
            edge.at[k], edge_in.at[k], e_s.at[k], e_r.at[k],
            device_id=greet[k], device_id_type=MESH,
        )
        for k in range(2)
    ]
    for copy in edges:
        copy.start()

    def source(q):
        return x.at[q, 1, pl.ds(mine, 8)]

    across = [
        pltpu.make_async_remote_copy(
            source(q), x.at[q, 1, pl.ds(mine, 8)], z_s.at[q], z_r.at[q],
            device_id={"stream": o}, device_id_type=MESH,
        )
        for q in range(NQ)
    ]

    def along(q, side, layers, send, recv):
        return pltpu.make_async_remote_copy(
            x.at[q, 1, pl.ds(layers, 8)], x.at[q, 2 * side, pl.ds(layers, 8)],
            send.at[q, side], recv.at[q, side],
            device_id=greet[2 + side], device_id_type=MESH,
        )

    def to_neighbours(method, q, layers, send, recv):
        for side in range(2):
            edge_of_wall = wl < nw - 1 if side == 0 else wl > 0

            @pl.when(edge_of_wall)
            def _(side=side):
                getattr(along(q, side, layers, send, recv), method)()

    def from_neighbours(q, layers, send, recv):
        for side in range(2):
            edge_of_wall = wl > 0 if side == 0 else wl < nw - 1

            @pl.when(edge_of_wall)
            def _(side=side):
                along(q, side, layers, send, recv).wait_recv()

    order = (3, 0, 1, 2, 4)
    for q in order[:4]:
        across[q].start()
    for q in order[:4]:
        to_neighbours("start", q, mine, own_s, own_r)

    for copy in edges:
        copy.wait_recv()
    before = edge_in[0].reshape(64, 128)
    after = edge_in[1].reshape(64, 128)
    left = lane % 32 < 16
    x[4, 1, pl.ds(mine, 8), 0:8, :] = jnp.where(left, before, after).reshape(8, 8, 128)
    x[4, 1, pl.ds(mine, 8), 8:16, :] = jnp.where(
        left, pltpu.roll(before, 112, 1), pltpu.roll(after, 16, 1)
    ).reshape(8, 8, 128)
    across[4].start()
    to_neighbours("start", 4, mine, own_s, own_r)

    def forward(q):
        across[q].wait_recv()
        to_neighbours("start", q, theirs, rel_s, rel_r)

    def plane_filter(q):
        from_neighbours(q, mine, own_s, own_r)
        from_neighbours(q, theirs, rel_s, rel_r)
        parts = [x[q, half : half + 2].reshape(512, 128) for half in range(2)]
        hi, lo = zip(*[hi_lo(part) for part in parts])
        hi, lo = jnp.concatenate(hi, axis=1), jnp.concatenate(lo, axis=1)
        y = jnp.dot(
            km[...], jnp.concatenate([hi, lo, hi], axis=0), preferred_element_type=F32
        )
        for half in range(2):
            hi, lo = hi_lo(y[:, 128 * half : 128 * half + 128])
            yh[q, 256 * half : 256 * half + 256, :] = hi
            yl[q, 256 * half : 256 * half + 256, :] = lo

    forward(order[0])
    local[4].wait()
    for at in range(1, NQ):
        forward(order[at])
        plane_filter(order[at - 1])
    plane_filter(order[NQ - 1])

    local[6].wait()
    rims = jnp.zeros((512, 128), F32)
    m[:, 0] = jnp.zeros((4, 32, 128), F32)
    m[:, 17] = jnp.zeros((4, 32, 128), F32)
    for f in range(4):
        hi = jnp.concatenate([yh[f], yh[4]], axis=1)
        lo = jnp.concatenate([yl[f], yl[4]], axis=1)
        out = jnp.dot(
            jnp.concatenate([hi, lo, hi], axis=1), wm[f], preferred_element_type=F32
        )
        for half in range(2):
            m[f, 1:17, 16 * half : 16 * half + 16, :] = out[
                256 * half : 256 * half + 256, :128
            ].reshape(16, 16, 128)
        rims = rims + out[:, 128:]
    for half in range(2):
        mh[:, 16 * half : 16 * half + 16, :] = rims[256 * half : 256 * half + 256].reshape(
            16, 16, 128
        )

    @pl.when(wl == 0)
    def _():
        m[:, :, 0:8, :] = jnp.zeros((4, 18, 8, 128), F32)
        mh[:, 0:8, :] = jnp.zeros((16, 8, 128), F32)

    @pl.when(wl == nw - 1)
    def _():
        m[:, :, 24:32, :] = jnp.zeros((4, 18, 8, 128), F32)
        mh[:, 24:32, :] = jnp.zeros((16, 8, 128), F32)

    local[5].wait()

    def window(q):
        return jnp.concatenate(
            [x[q, 0, :, 8:16, :], x[q, 1], x[q, 2, :, 0:8, :]], axis=1
        ).reshape(512, 128)

    def own_plane(values):
        hi, lo = hi_lo(values)
        return jnp.dot(
            ko[...], jnp.concatenate([hi, lo, hi], axis=0), preferred_element_type=F32
        )

    def own_span(f, body, rim):
        hi, lo = hi_lo(jnp.concatenate([body, rim], axis=1))
        return jnp.dot(
            jnp.concatenate([hi, lo, hi], axis=1),
            wm[f, :, 0:128],
            preferred_element_type=F32,
        )

    scalar_x = window(3)
    first_rim = own_plane(rim_product(window(4)))
    first = [own_span(i, own_plane(window(i) * scalar_x), first_rim) for i in range(3)]

    inner = pl.ds(1 + s * 8, 8)
    means = [m[f, 1:17].reshape(512, 128) for f in range(4)]
    mean_rim = mh[...].reshape(512, 128)
    second_rim = own_plane(mean_rim)
    second = [own_span(f, own_plane(means[f]), second_rim) for f in range(4)]
    flux_rim = own_plane(rim_product(mean_rim))
    flux = [own_span(i, own_plane(means[i] * means[3]), flux_rim) for i in range(3)]

    lane = lax.broadcasted_iota(jnp.int32, (128, 128), 1)
    own_rim = mh[pl.ds(mine, 8), 8:24, :].reshape(128, 128)
    own, slopes = [], []
    for f in range(4):
        c = m[f, inner, 8:24, :].reshape(128, 128)
        up = pltpu.roll(c, 127, 1)
        up = jnp.where(lane == 127, pltpu.roll(own_rim, (127 - (f * 32 + 16)) % 128, 1), up)
        down = pltpu.roll(c, 1, 1)
        down = jnp.where(lane == 0, pltpu.roll(own_rim, (128 - (f * 32 + 15)) % 128, 1), down)
        along_wall = m[f, inner, 9:25, :] - m[f, inner, 7:23, :]
        along_stream = m[f, pl.ds(2 + s * 8, 8), 8:24, :] - m[f, pl.ds(s * 8, 8), 8:24, :]
        own.append(c)
        slopes.append(
            (
                (up - down) * 0.5,
                along_wall.reshape(128, 128) * 0.5,
                along_stream.reshape(128, 128) * 0.5,
            )
        )

    clarks, similars = [], []
    ones = jnp.ones((8, 128), F32)
    sums = [[] for _ in range(5)]
    for i in range(3):
        exact = first[i] - own[i] * own[3]
        similar = flux[i] - second[i] * second[3]
        total = slopes[i][0] * slopes[3][0] + slopes[i][1] * slopes[3][1]
        clark = clark_coef * (total + slopes[i][2] * slopes[3][2])
        clarks.append(clark)
        similars.append(similar)
        pairs = (
            (exact, clark), (exact, similar), (exact, exact), (clark, clark), (similar, similar)
        )
        for k, (a, b) in enumerate(pairs):
            sums[k].append(jnp.sum((a * b).reshape(8, 16, 128), axis=0))
    st[...] = jnp.zeros((8, 128), F32)
    for k in range(5):
        rows = jnp.concatenate(sums[k], axis=0)
        got = lax.dot_general(
            ones, rows, (((1,), (1,)), ((), ())),
            precision=lax.Precision.HIGHEST, preferred_element_type=F32,
        )
        st[k : k + 1, 0:48] = got[0:1, :]

    group = xi * 2 + s
    st_a[group] = st[...]
    sends = [
        pltpu.make_async_remote_copy(
            st, st_a.at[group], a_s.at[k], a_r.at[k],
            device_id=row_mates[k], device_id_type=MESH,
        )
        for k in range(len(row_mates))
    ]
    for copy in sends:
        copy.start()
    for copy in sends:
        copy.wait_recv()
    total = st_a[0]
    for k in range(1, 2 * ROW):
        total = total + st_a[k]
    st_t[...] = total
    st_b[zi] = total
    more = [
        pltpu.make_async_remote_copy(
            st_t, st_b.at[zi], b_s.at[k], b_r.at[k],
            device_id=col_mates[k], device_id_type=MESH,
        )
        for k in range(len(col_mates))
    ]
    for copy in more:
        copy.start()
    for copy in more:
        copy.wait_recv()
    total = st_b[0]
    for k in range(1, nz):
        total = total + st_b[k]
    total = total[:, 0:48] / cells

    power_e, power_c, power_s = total[2:3], total[3:4], total[4:5]
    clark_corr = total[0:1] / jnp.sqrt((power_e + small_eps) * (power_c + small_eps))
    similar_corr = total[1:2] / jnp.sqrt((power_e + small_eps) * (power_s + small_eps))
    for i in range(3):
        cc_out[i : i + 1, :] = clark_corr[:, 16 * i : 16 * i + 16]
        sc_out[i : i + 1, :] = similar_corr[:, 16 * i : 16 * i + 16]
    spot = lax.broadcasted_iota(jnp.int32, (48, 48), 0) == lax.broadcasted_iota(
        jnp.int32, (48, 48), 1
    )
    for power, values, out in (
        (power_c, clarks, clark_out), (power_s, similars, similar_out)
    ):
        scale = 1.0 / jnp.sqrt(power + small_eps)
        scale = jnp.sum(
            jnp.where(spot, jnp.broadcast_to(scale, (48, 48)), 0.0), axis=1, keepdims=True
        )
        for i in range(3):
            rows = jnp.broadcast_to(scale[16 * i : 16 * i + 16], (16, 128))
            out[i] = values[i].reshape(8, 16, 128) * rows[None]

    for copy in edges + across + sends + more:
        copy.wait_send()
    for q in range(NQ):
        to_neighbours("wait_send", q, mine, own_s, own_r)
        to_neighbours("wait_send", q, theirs, rel_s, rel_r)


def shards(fields):
    nz = lax.axis_size("span") // ROW
    cells = float(
        fields.shape[1] * fields.shape[3] * lax.axis_size("stream") * lax.axis_size("span")
    )
    km, ko = plane_matrices()
    wm = span_matrices()
    vmem = pl.BlockSpec(memory_space=pltpu.VMEM)
    hbm = pl.BlockSpec(memory_space=pl.ANY)
    dma = pltpu.SemaphoreType.DMA

    def body(*refs):
        kernel(cells, *refs)

    return pl.pallas_call(
        body,
        out_shape=(
            jax.ShapeDtypeStruct((3, 8, 16, 128), F32),
            jax.ShapeDtypeStruct((3, 8, 16, 128), F32),
            jax.ShapeDtypeStruct((3, 16), F32),
            jax.ShapeDtypeStruct((3, 16), F32),
        ),
        in_specs=[hbm] * 4,
        out_specs=(vmem, vmem, vmem, vmem),
        scratch_shapes=[
            pltpu.VMEM((NQ, 3, 16, 16, 128), F32),
            pltpu.VMEM((2, 8, 8, 128), F32),
            pltpu.VMEM((2, 8, 8, 128), F32),
            pltpu.VMEM((256, 1536), BF),
            pltpu.VMEM((128, 1536), BF),
            pltpu.VMEM((4, 768, 256), BF),
            pltpu.VMEM((NQ, 512, 128), BF),
            pltpu.VMEM((NQ, 512, 128), BF),
            pltpu.VMEM((4, 18, 32, 128), F32),
            pltpu.VMEM((16, 32, 128), F32),
            pltpu.VMEM((8, 128), F32),
            pltpu.VMEM((8, 128), F32),
            pltpu.VMEM((2 * ROW, 8, 128), F32),
            pltpu.VMEM((8, 128), F32),
            pltpu.VMEM((nz, 8, 128), F32),
            dma((7,)),
            dma((NQ,)), dma((NQ,)),
            dma((NQ, 2)), dma((NQ, 2)),
            dma((NQ, 2)), dma((NQ, 2)),
            dma((2,)), dma((2,)),
            dma((2 * ROW - 1,)), dma((2 * ROW - 1,)),
            dma((max(nz - 1, 1),)), dma((max(nz - 1, 1),)),
        ],
        compiler_params=pltpu.CompilerParams(
            collective_id=0, has_side_effects=True, vmem_limit_bytes=48 * 2**20
        ),
        cost_estimate=pl.CostEstimate(
            flops=8_000_000_000, bytes_accessed=4_000_000, transcendentals=0
        ),
    )(fields, jnp.asarray(km), jnp.asarray(ko), jnp.asarray(wm))


def solution(mesh):
    return jax.shard_map(
        shards,
        mesh=mesh,
        in_specs=(P(None, "stream", "wall", "span"),),
        out_specs=(
            P(None, "stream", "wall", "span"),
            P(None, "stream", "wall", "span"),
            P(None, "wall"),
            P(None, "wall"),
        ),
        check_vma=False,
    )
```

time: 372 us -> 52.6 us (0.14)
  the two profiles are of different devices: /device:TPU:16 before, /device:TPU:25 now
where the time goes in v1:
time: 52.6 us; the launch traced here: 52.4 us
  Pallas kernels  44.6 us (85%)
  local copies, waits for them, and re-layouts  7.13 us (14%)
  between operations  0.65 us (1%)
    pallas_call x1, Pallas kernels, shards(): pl.pallas_call(body, out_shape=(jax.ShapeDtypeStruct((3, 8, 16, 128), F32...  44.6 us
    unnamed x12, local copies, waits for them, and re-layouts  7.13 us

profile of v1, /device:TPU:25, one launch (start us, length us, event | category | flops | bytes accessed | tf_op | source)
XLA Modules:
  0.0 52.4 jit_solution(5553283529443207538)
XLA Ops:
  0.6 0.0 copy-start
  0.6 0.9 %copy-done = f32[4,8,16,128]{3,2,1,0:T(8,128)S(1)} copy-done((f32[4,8,16,128]{3,2,1,0:T(8,128)S(1)}, f32[4,8,16,128]{3,2,1,0:T(8,128)}, u32[]{:S(2)}) %copy-start) | copy-done | bytes 262168
  1.6 0.0 copy-start.1
  1.6 1.4 %copy-done.1 = bf16[4,768,256]{2,1,0:T(8,128)(2,1)S(1)} copy-done((bf16[4,768,256]{2,1,0:T(8,128)(2,1)S(1)}, bf16[4,768,256]{2,1,0:T(8,128)(2,1)}, u32[]{:S(2)}) %copy-start.1) | copy-done | bytes 1572888
  3.0 0.0 copy-start.2
  3.0 1.1 %copy-done.2 = bf16[2,128,1536]{2,1,0:T(8,128)(2,1)S(1)} copy-done((bf16[2,128,1536]{2,1,0:T(8,128)(2,1)S(1)}, bf16[2,128,1536]{2,1,0:T(8,128)(2,1)}, u32[]{:S(2)}) %copy-start.2) | copy-done | bytes 786456
  4.1 0.0 copy-start.3
  4.1 1.1 %copy-done.3 = bf16[256,1536]{1,0:T(8,128)(2,1)S(1)} copy-done((bf16[256,1536]{1,0:T(8,128)(2,1)S(1)}, bf16[256,1536]{1,0:T(8,128)(2,1)}, u32[]{:S(2)}) %copy-start.3) | copy-done | bytes 786456
  5.3 44.6 %shard_map.75 = (f32[3,8,16,128]{3,2,1,0:T(8,128)S(1)}, f32[3,8,16,128]{3,2,1,0:T(8,128)S(1)}, f32[3,16]{1,0:T(4,128)S(1)}, f32[3,16]{1,0:T(4,128)S(1)}) custom-call(f32[4,8,16,128]{3,2,1,0:T(8,128)S(1)} %copy-done, bf16[256,1536]{1,0:T(8,128)(2,1)S(1)} %copy-done.3, bf16[2,128,1536]{2,1,0:T(8,128)(2,1)S(1)} %copy-done.2, bf16[4,768,256]{2,1,0:T(8,128)(2,1)S(1)} %copy-done.1), custom_call_target="tpu_custom_call" | custom-call | flops 8000000000 | bytes 4000000 | tf_op jit(solution)/shard_map/pallas_call | solution.py:423
  49.9 0.7 %copy.12 = f32[3,8,16,128]{3,2,1,0:T(8,128)} copy(f32[3,8,16,128]{3,2,1,0:T(8,128)S(1)} %get-tuple-element.8) | data formatting | bytes 393216
  50.5 0.7 %copy.13 = f32[3,8,16,128]{3,2,1,0:T(8,128)} copy(f32[3,8,16,128]{3,2,1,0:T(8,128)S(1)} %get-tuple-element.9) | data formatting | bytes 393216
  51.2 0.6 %copy.14 = f32[3,16]{1,0:T(4,128)} copy(f32[3,16]{1,0:T(4,128)S(1)} %get-tuple-element.10) | data formatting | bytes 384
  51.8 0.6 %copy.15 = f32[3,16]{1,0:T(4,128)} copy(f32[3,16]{1,0:T(4,128)S(1)} %get-tuple-element.11) | data formatting | bytes 384
Async XLA Ops:
  0.6 1.0 %copy-start = (f32[4,8,16,128]{3,2,1,0:T(8,128)S(1)}, f32[4,8,16,128]{3,2,1,0:T(8,128)}, u32[]{:S(2)}) copy-start(f32[4,8,16,128]{3,2,1,0:T(8,128)} %refs_0_.1) | copy-start | bytes 786436
  1.6 1.4 %copy-start.1 = (bf16[4,768,256]{2,1,0:T(8,128)(2,1)S(1)}, bf16[4,768,256]{2,1,0:T(8,128)(2,1)}, u32[]{:S(2)}) copy-start(bf16[4,768,256]{2,1,0:T(8,128)(2,1)} %constant.8.clone.refs_3_) | copy-start | bytes 4718596
  3.0 1.1 %copy-start.2 = (bf16[2,128,1536]{2,1,0:T(8,128)(2,1)S(1)}, bf16[2,128,1536]{2,1,0:T(8,128)(2,1)}, u32[]{:S(2)}) copy-start(bf16[2,128,1536]{2,1,0:T(8,128)(2,1)} %constant.7.clone.refs_2_) | copy-start | bytes 2359300
  4.1 1.1 %copy-start.3 = (bf16[256,1536]{1,0:T(8,128)(2,1)S(1)}, bf16[256,1536]{1,0:T(8,128)(2,1)}, u32[]{:S(2)}) copy-start(bf16[256,1536]{1,0:T(8,128)(2,1)} %constant.6.clone.refs_1_) | copy-start | bytes 2359300

commit v2 on v1

--- a/solution.py
+++ b/solution.py
@@ -85,9 +85,9 @@
 
 
 def kernel(
-    cells, fields, km_in, ko_in, w_in,
-    clark_out, similar_out, cc_out, sc_out,
-    x, edge, edge_in, km, ko, wm, yh, yl, m, mh, zs, st, st_a, st_t, st_b,
+    fields, km_in, ko_in, w_in,
+    clark_out, similar_out, sums_out,
+    x, edge, edge_in, km, ko, wm, yh, yl, m, mh, st, st_a, st_t, st_b,
     loc, z_s, z_r, own_s, own_r, rel_s, rel_r, e_s, e_r, a_s, a_r, b_s, b_r,
 ):
     p, wl, s = lax.axis_index("span"), lax.axis_index("wall"), lax.axis_index("stream")
@@ -321,7 +321,6 @@
             )
         )
 
-    clarks, similars = [], []
     ones = jnp.ones((8, 128), F32)
     sums = [[] for _ in range(5)]
     for i in range(3):
@@ -329,8 +328,8 @@
         similar = flux[i] - second[i] * second[3]
         total = slopes[i][0] * slopes[3][0] + slopes[i][1] * slopes[3][1]
         clark = clark_coef * (total + slopes[i][2] * slopes[3][2])
-        clarks.append(clark)
-        similars.append(similar)
+        clark_out[i] = clark.reshape(8, 16, 128)
+        similar_out[i] = similar.reshape(8, 16, 128)
         pairs = (
             (exact, clark), (exact, similar), (exact, exact), (clark, clark), (similar, similar)
         )
@@ -377,33 +376,50 @@
     total = st_b[0]
     for k in range(1, nz):
         total = total + st_b[k]
-    total = total[:, 0:48] / cells
-
-    power_e, power_c, power_s = total[2:3], total[3:4], total[4:5]
-    clark_corr = total[0:1] / jnp.sqrt((power_e + small_eps) * (power_c + small_eps))
-    similar_corr = total[1:2] / jnp.sqrt((power_e + small_eps) * (power_s + small_eps))
-    for i in range(3):
-        cc_out[i : i + 1, :] = clark_corr[:, 16 * i : 16 * i + 16]
-        sc_out[i : i + 1, :] = similar_corr[:, 16 * i : 16 * i + 16]
-    spot = lax.broadcasted_iota(jnp.int32, (48, 48), 0) == lax.broadcasted_iota(
-        jnp.int32, (48, 48), 1
-    )
-    for power, values, out in (
-        (power_c, clarks, clark_out), (power_s, similars, similar_out)
-    ):
-        scale = 1.0 / jnp.sqrt(power + small_eps)
-        scale = jnp.sum(
-            jnp.where(spot, jnp.broadcast_to(scale, (48, 48)), 0.0), axis=1, keepdims=True
-        )
-        for i in range(3):
-            rows = jnp.broadcast_to(scale[16 * i : 16 * i + 16], (16, 128))
-            out[i] = values[i].reshape(8, 16, 128) * rows[None]
+    sums_out[...] = total
 
     for copy in edges + across + sends + more:
         copy.wait_send()
     for q in range(NQ):
         to_neighbours("wait_send", q, mine, own_s, own_r)
         to_neighbours("wait_send", q, theirs, rel_s, rel_r)
+
+
+def finish(
+    cells, clark, similar, sums, clark_out, similar_out, cc_out, sc_out,
+    c_buf, s_buf, cc_buf, sc_buf, sem,
+):
+    total = sums[:, 0:48] / cells
+    power_e, power_c, power_s = total[2:3], total[3:4], total[4:5]
+    clark_corr = total[0:1] / jnp.sqrt((power_e + small_eps) * (power_c + small_eps))
+    similar_corr = total[1:2] / jnp.sqrt((power_e + small_eps) * (power_s + small_eps))
+    copies = []
+
+    def send(src, dst):
+        copy = pltpu.make_async_copy(src, dst, sem.at[len(copies)])
+        copy.start()
+        copies.append(copy)
+
+    spot = lax.broadcasted_iota(jnp.int32, (48, 48), 0) == lax.broadcasted_iota(
+        jnp.int32, (48, 48), 1
+    )
+    for power, values, buf, out in (
+        (power_c, clark, c_buf, clark_out), (power_s, similar, s_buf, similar_out)
+    ):
+        scale = 1.0 / jnp.sqrt(power + small_eps)
+        scale = jnp.sum(
+            jnp.where(spot, jnp.broadcast_to(scale, (48, 48)), 0.0), axis=1, keepdims=True
+        )
+        for i in range(3):
+            rows = jnp.broadcast_to(scale[16 * i : 16 * i + 16], (16, 128))
+            buf[i] = values[i] * rows[None]
+            send(buf.at[i], out.at[i])
+    for corr, buf, out in ((clark_corr, cc_buf, cc_out), (similar_corr, sc_buf, sc_out)):
+        for i in range(3):
+            buf[i : i + 1, :] = corr[:, 16 * i : 16 * i + 16]
+        send(buf, out)
+    for copy in copies:
+        copy.wait()
 
 
 def shards(fields):
@@ -414,22 +430,16 @@
     km, ko = plane_matrices()
     wm = span_matrices()
     vmem = pl.BlockSpec(memory_space=pltpu.VMEM)
-    hbm = pl.BlockSpec(memory_space=pl.ANY)
+    hbm = pl.BlockSpec(memory_space=pltpu.HBM)
     dma = pltpu.SemaphoreType.DMA
 
-    def body(*refs):
-        kernel(cells, *refs)
-
-    return pl.pallas_call(
-        body,
-        out_shape=(
-            jax.ShapeDtypeStruct((3, 8, 16, 128), F32),
-            jax.ShapeDtypeStruct((3, 8, 16, 128), F32),
-            jax.ShapeDtypeStruct((3, 16), F32),
-            jax.ShapeDtypeStruct((3, 16), F32),
-        ),
+    flux = jax.ShapeDtypeStruct((3, 8, 16, 128), F32)
+    corr = jax.ShapeDtypeStruct((3, 16), F32)
+    clark, similar, sums = pl.pallas_call(
+        kernel,
+        out_shape=(flux, flux, jax.ShapeDtypeStruct((8, 128), F32)),
         in_specs=[hbm] * 4,
-        out_specs=(vmem, vmem, vmem, vmem),
+        out_specs=(vmem, vmem, vmem),
         scratch_shapes=[
             pltpu.VMEM((NQ, 3, 16, 16, 128), F32),
             pltpu.VMEM((2, 8, 8, 128), F32),
@@ -441,7 +451,6 @@
             pltpu.VMEM((NQ, 512, 128), BF),
             pltpu.VMEM((4, 18, 32, 128), F32),
             pltpu.VMEM((16, 32, 128), F32),
-            pltpu.VMEM((8, 128), F32),
             pltpu.VMEM((8, 128), F32),
             pltpu.VMEM((2 * ROW, 8, 128), F32),
             pltpu.VMEM((8, 128), F32),
@@ -455,12 +464,30 @@
             dma((max(nz - 1, 1),)), dma((max(nz - 1, 1),)),
         ],
         compiler_params=pltpu.CompilerParams(
-            collective_id=0, has_side_effects=True, vmem_limit_bytes=48 * 2**20
+            collective_id=0, has_side_effects=True, vmem_limit_bytes=54680 * 2**10
         ),
         cost_estimate=pl.CostEstimate(
             flops=8_000_000_000, bytes_accessed=4_000_000, transcendentals=0
         ),
     )(fields, jnp.asarray(km), jnp.asarray(ko), jnp.asarray(wm))
+
+    def last(*refs):
+        finish(cells, *refs)
+
+    return pl.pallas_call(
+        last,
+        out_shape=(flux, flux, corr, corr),
+        in_specs=[vmem] * 3,
+        out_specs=(hbm, hbm, hbm, hbm),
+        scratch_shapes=[
+            pltpu.VMEM((3, 8, 16, 128), F32),
+            pltpu.VMEM((3, 8, 16, 128), F32),
+            pltpu.VMEM((3, 16), F32),
+            pltpu.VMEM((3, 16), F32),
+            dma((8,)),
+        ],
+        compiler_params=pltpu.CompilerParams(vmem_limit_bytes=8 * 2**20),
+    )(clark, similar, sums)
 
 
 def solution(mesh):

time: 52.6 us -> 45.5 us (0.87)
  local copies, waits for them, and re-layouts: 7.13 us -> 0 us
    unnamed x12 -> x0, local copies, waits for them, and re-layouts: 7.13 us -> none
    pallas_call x1 -> x2, Pallas kernels: 44.6 us -> 44.7 us  [the longest x1 43.8 us: shards(): pl.pallas_call(kernel, out_shape=(flux, flux, jax.ShapeDtypeStruct((8, 12...]
where the time goes in v2:
time: 45.5 us; the launch traced here: 45.4 us
  Pallas kernels  44.7 us (98%)
  between operations  0.64 us (1%)
    pallas_call x1, Pallas kernels, shards(): pl.pallas_call(kernel, out_shape=(flux, flux, jax.ShapeDtypeStruct((8, 12...  43.8 us
    pallas_call x1, Pallas kernels, shards(): pl.pallas_call(last, out_shape=(flux, flux, corr, corr), in_specs=[vmem]...  0.91 us

profile of v2, /device:TPU:25, one launch (start us, length us, event | category | flops | bytes accessed | tf_op | source)
XLA Modules:
  0.0 45.4 jit_solution(8131136057308693368)
XLA Ops:
  0.6 43.8 %shard_map.75 = (f32[3,8,16,128]{3,2,1,0:T(8,128)S(1)}, f32[3,8,16,128]{3,2,1,0:T(8,128)S(1)}, f32[8,128]{1,0:T(8,128)S(1)}) custom-call(f32[4,8,16,128]{3,2,1,0:T(8,128)} %fields.1, bf16[256,1536]{1,0:T(8,128)(2,1)} %constant.6.clone.km_in, bf16[2,128,1536]{2,1,0:T(8,128)(2,1)} %constant.7.clone.ko_in, bf16[4,768,256]{2,1,0:T(8,128)(2,1)} %constant.8.clone.w_in), custom_call_target="tpu_custom_call" | custom-call | flops 8000000000 | bytes 4000000 | tf_op jit(solution)/shard_map/pallas_call | solution.py:438
  44.4 0.9 %shard_map.76 = (f32[3,8,16,128]{3,2,1,0:T(8,128)}, f32[3,8,16,128]{3,2,1,0:T(8,128)}, f32[3,16]{1,0:T(4,128)}, f32[3,16]{1,0:T(4,128)}) custom-call(f32[3,8,16,128]{3,2,1,0:T(8,128)S(1)} %get-tuple-element.7.refs_0_, f32[3,8,16,128]{3,2,1,0:T(8,128)S(1)} %get-tuple-element.8.refs_1_, f32[8,128]{1,0:T(8,128)S(1)} %get-tuple-element.9.refs_2_), custom_call_target="tpu_custom_call" | custom-call | tf_op jit(solution)/shard_map/pallas_call | solution.py:477

commit v3 on v2

--- a/solution.py
+++ b/solution.py
@@ -65,8 +65,8 @@
     for f in range(4):
         from_rim = tap(lane[None, :], place[:, None]) * (group == f)[:, None]
         to_rim = tap(place[None, :], lane[:, None]) * ((group == f) & kept)[None, :]
-        rim = tap(place[None, :], place[:, None]) * (group[:, None] == group[None, :])
-        rim = rim * kept[None, :] * (1.0 if f == 0 else 0.0)
+        rim = tap(place[None, :], place[:, None]) * (group == f)[:, None]
+        rim = rim * ((group == f) & kept)[None, :]
         result.append(right_stack(np.block([[main, to_rim], [from_rim, rim]])))
     return np.stack(result)
 
@@ -195,11 +195,124 @@
             def _(side=side):
                 along(q, side, layers, send, recv).wait_recv()
 
-    order = (3, 0, 1, 2, 4)
-    for q in order[:4]:
+    def send_own(q):
         across[q].start()
-    for q in order[:4]:
         to_neighbours("start", q, mine, own_s, own_r)
+
+    def forward(q):
+        across[q].wait_recv()
+        to_neighbours("start", q, theirs, rel_s, rel_r)
+
+    def plane_filter(q):
+        from_neighbours(q, mine, own_s, own_r)
+        from_neighbours(q, theirs, rel_s, rel_r)
+        blocks = [hi_lo(x[q, b].reshape(256, 128)) for b in range(3)]
+
+        def pair(k):
+            return jnp.concatenate(
+                [
+                    jnp.concatenate([blocks[0][k], blocks[1][k]], axis=0),
+                    jnp.concatenate([blocks[1][k], blocks[2][k]], axis=0),
+                ],
+                axis=1,
+            )
+
+        hi, lo = pair(0), pair(1)
+        y = jnp.dot(
+            km[...], jnp.concatenate([hi, lo, hi], axis=0), preferred_element_type=F32
+        )
+        for half in range(2):
+            hi, lo = hi_lo(y[:, 128 * half : 128 * half + 128])
+            yh[q, 256 * half : 256 * half + 256, :] = hi
+            yl[q, 256 * half : 256 * half + 256, :] = lo
+
+    low = jnp.where(wl > 0, 1.0, 0.0)
+    high = jnp.where(wl < nw - 1, 1.0, 0.0)
+
+    def mean_field(f):
+        hi = jnp.concatenate([yh[f], yh[4]], axis=1)
+        lo = jnp.concatenate([yl[f], yl[4]], axis=1)
+        out = jnp.dot(
+            jnp.concatenate([hi, lo, hi], axis=1), wm[f], preferred_element_type=F32
+        ).reshape(2, 16, 16, 256)
+        parts = (out[0, :, 0:8] * low, out[0, :, 8:16], out[1, :, 0:8], out[1, :, 8:16] * high)
+        for k in range(4):
+            m[f, 1:17, 8 * k : 8 * k + 8, :] = parts[k][:, :, :128]
+            mh[f, :, 8 * k : 8 * k + 8, :] = parts[k][:, :, 128:]
+
+    def window(q):
+        return jnp.concatenate(
+            [x[q, 0, :, 8:16, :], x[q, 1], x[q, 2, :, 0:8, :]], axis=1
+        ).reshape(512, 128)
+
+    def own_plane(values):
+        hi, lo = hi_lo(jnp.concatenate(values, axis=1))
+        out = jnp.dot(
+            ko[...], jnp.concatenate([hi, lo, hi], axis=0), preferred_element_type=F32
+        )
+        return [out[:, 128 * k : 128 * k + 128] for k in range(len(values))]
+
+    def own_span(f, bodies, rims):
+        rows = [jnp.concatenate(pair, axis=1) for pair in zip(bodies, rims)]
+        hi, lo = hi_lo(jnp.concatenate(rows, axis=0))
+        out = jnp.dot(
+            jnp.concatenate([hi, lo, hi], axis=1),
+            wm[f, :, 0:128],
+            preferred_element_type=F32,
+        )
+        return [out[128 * k : 128 * k + 128] for k in range(len(bodies))]
+
+    inner = pl.ds(1 + s * 8, 8)
+    wide = lax.broadcasted_iota(jnp.int32, (128, 128), 1)
+
+    def own_mean(f):
+        c = m[f, inner, 8:24, :].reshape(128, 128)
+        rim = mh[f, pl.ds(mine, 8), 8:24, :].reshape(128, 128)
+        up = pltpu.roll(c, 127, 1)
+        up = jnp.where(wide == 127, pltpu.roll(rim, (127 - (f * 32 + 16)) % 128, 1), up)
+        down = pltpu.roll(c, 1, 1)
+        down = jnp.where(wide == 0, pltpu.roll(rim, (128 - (f * 32 + 15)) % 128, 1), down)
+        along_wall = m[f, inner, 9:25, :] - m[f, inner, 7:23, :]
+        along_stream = m[f, pl.ds(2 + s * 8, 8), 8:24, :] - m[f, pl.ds(s * 8, 8), 8:24, :]
+        return c, (
+            (up - down) * 0.5,
+            along_wall.reshape(128, 128) * 0.5,
+            along_stream.reshape(128, 128) * 0.5,
+        )
+
+    def flat_mean(f):
+        return m[f, 1:17].reshape(512, 128), mh[f].reshape(512, 128)
+
+    ones = jnp.ones((8, 128), F32)
+
+    def component(i, first_rim, second_t, own_t, slopes_t):
+        mean, rim = flat_mean(i)
+        mean_t, rim_t = flat_mean(3)
+        shift = (32 * i - 96) % 128
+        product_rim = rim * pltpu.roll(rim_t, shift, 1)
+        both = rim + pltpu.roll(product_rim, (128 - shift) % 128, 1)
+        z_x, z_m, z_p, z_r = own_plane([window(i) * window(3), mean, mean * mean_t, both])
+        first, second = own_span(i, [z_x, z_m], [first_rim, z_r])
+        (flux,) = own_span(3, [z_p], [z_r])
+        own, slopes = own_mean(i)
+        exact = first - own * own_t
+        similar = flux - second * second_t
+        total = slopes[0] * slopes_t[0] + slopes[1] * slopes_t[1]
+        clark = clark_coef * (total + slopes[2] * slopes_t[2])
+        clark_out[i] = clark.reshape(8, 16, 128)
+        similar_out[i] = similar.reshape(8, 16, 128)
+        pairs = (
+            (exact, clark), (exact, similar), (exact, exact), (clark, clark), (similar, similar)
+        )
+        rows = [jnp.sum((a * b).reshape(8, 16, 128), axis=0) for a, b in pairs]
+        got = lax.dot_general(
+            ones, jnp.concatenate(rows, axis=0), (((1,), (1,)), ((), ())),
+            precision=lax.Precision.HIGHEST, preferred_element_type=F32,
+        )
+        st[i : i + 1, 0:80] = got[0:1, :]
+
+    send_own(3)
+    send_own(0)
 
     for copy in edges:
         copy.wait_recv()
@@ -210,139 +323,35 @@
     x[4, 1, pl.ds(mine, 8), 8:16, :] = jnp.where(
         left, pltpu.roll(before, 112, 1), pltpu.roll(after, 16, 1)
     ).reshape(8, 8, 128)
-    across[4].start()
-    to_neighbours("start", 4, mine, own_s, own_r)
-
-    def forward(q):
-        across[q].wait_recv()
-        to_neighbours("start", q, theirs, rel_s, rel_r)
-
-    def plane_filter(q):
-        from_neighbours(q, mine, own_s, own_r)
-        from_neighbours(q, theirs, rel_s, rel_r)
-        parts = [x[q, half : half + 2].reshape(512, 128) for half in range(2)]
-        hi, lo = zip(*[hi_lo(part) for part in parts])
-        hi, lo = jnp.concatenate(hi, axis=1), jnp.concatenate(lo, axis=1)
-        y = jnp.dot(
-            km[...], jnp.concatenate([hi, lo, hi], axis=0), preferred_element_type=F32
-        )
-        for half in range(2):
-            hi, lo = hi_lo(y[:, 128 * half : 128 * half + 128])
-            yh[q, 256 * half : 256 * half + 256, :] = hi
-            yl[q, 256 * half : 256 * half + 256, :] = lo
-
-    forward(order[0])
-    local[4].wait()
-    for at in range(1, NQ):
-        forward(order[at])
-        plane_filter(order[at - 1])
-    plane_filter(order[NQ - 1])
-
-    local[6].wait()
-    rims = jnp.zeros((512, 128), F32)
+    send_own(4)
+    send_own(1)
+    send_own(2)
+
+    st[...] = jnp.zeros((8, 128), F32)
     m[:, 0] = jnp.zeros((4, 32, 128), F32)
     m[:, 17] = jnp.zeros((4, 32, 128), F32)
-    for f in range(4):
-        hi = jnp.concatenate([yh[f], yh[4]], axis=1)
-        lo = jnp.concatenate([yl[f], yl[4]], axis=1)
-        out = jnp.dot(
-            jnp.concatenate([hi, lo, hi], axis=1), wm[f], preferred_element_type=F32
-        )
-        for half in range(2):
-            m[f, 1:17, 16 * half : 16 * half + 16, :] = out[
-                256 * half : 256 * half + 256, :128
-            ].reshape(16, 16, 128)
-        rims = rims + out[:, 128:]
-    for half in range(2):
-        mh[:, 16 * half : 16 * half + 16, :] = rims[256 * half : 256 * half + 256].reshape(
-            16, 16, 128
-        )
-
-    @pl.when(wl == 0)
-    def _():
-        m[:, :, 0:8, :] = jnp.zeros((4, 18, 8, 128), F32)
-        mh[:, 0:8, :] = jnp.zeros((16, 8, 128), F32)
-
-    @pl.when(wl == nw - 1)
-    def _():
-        m[:, :, 24:32, :] = jnp.zeros((4, 18, 8, 128), F32)
-        mh[:, 24:32, :] = jnp.zeros((16, 8, 128), F32)
-
+    forward(3)
+    forward(0)
+    local[4].wait()
     local[5].wait()
-
-    def window(q):
-        return jnp.concatenate(
-            [x[q, 0, :, 8:16, :], x[q, 1], x[q, 2, :, 0:8, :]], axis=1
-        ).reshape(512, 128)
-
-    def own_plane(values):
-        hi, lo = hi_lo(values)
-        return jnp.dot(
-            ko[...], jnp.concatenate([hi, lo, hi], axis=0), preferred_element_type=F32
-        )
-
-    def own_span(f, body, rim):
-        hi, lo = hi_lo(jnp.concatenate([body, rim], axis=1))
-        return jnp.dot(
-            jnp.concatenate([hi, lo, hi], axis=1),
-            wm[f, :, 0:128],
-            preferred_element_type=F32,
-        )
-
-    scalar_x = window(3)
-    first_rim = own_plane(rim_product(window(4)))
-    first = [own_span(i, own_plane(window(i) * scalar_x), first_rim) for i in range(3)]
-
-    inner = pl.ds(1 + s * 8, 8)
-    means = [m[f, 1:17].reshape(512, 128) for f in range(4)]
-    mean_rim = mh[...].reshape(512, 128)
-    second_rim = own_plane(mean_rim)
-    second = [own_span(f, own_plane(means[f]), second_rim) for f in range(4)]
-    flux_rim = own_plane(rim_product(mean_rim))
-    flux = [own_span(i, own_plane(means[i] * means[3]), flux_rim) for i in range(3)]
-
-    lane = lax.broadcasted_iota(jnp.int32, (128, 128), 1)
-    own_rim = mh[pl.ds(mine, 8), 8:24, :].reshape(128, 128)
-    own, slopes = [], []
-    for f in range(4):
-        c = m[f, inner, 8:24, :].reshape(128, 128)
-        up = pltpu.roll(c, 127, 1)
-        up = jnp.where(lane == 127, pltpu.roll(own_rim, (127 - (f * 32 + 16)) % 128, 1), up)
-        down = pltpu.roll(c, 1, 1)
-        down = jnp.where(lane == 0, pltpu.roll(own_rim, (128 - (f * 32 + 15)) % 128, 1), down)
-        along_wall = m[f, inner, 9:25, :] - m[f, inner, 7:23, :]
-        along_stream = m[f, pl.ds(2 + s * 8, 8), 8:24, :] - m[f, pl.ds(s * 8, 8), 8:24, :]
-        own.append(c)
-        slopes.append(
-            (
-                (up - down) * 0.5,
-                along_wall.reshape(128, 128) * 0.5,
-                along_stream.reshape(128, 128) * 0.5,
-            )
-        )
-
-    ones = jnp.ones((8, 128), F32)
-    sums = [[] for _ in range(5)]
-    for i in range(3):
-        exact = first[i] - own[i] * own[3]
-        similar = flux[i] - second[i] * second[3]
-        total = slopes[i][0] * slopes[3][0] + slopes[i][1] * slopes[3][1]
-        clark = clark_coef * (total + slopes[i][2] * slopes[3][2])
-        clark_out[i] = clark.reshape(8, 16, 128)
-        similar_out[i] = similar.reshape(8, 16, 128)
-        pairs = (
-            (exact, clark), (exact, similar), (exact, exact), (clark, clark), (similar, similar)
-        )
-        for k, (a, b) in enumerate(pairs):
-            sums[k].append(jnp.sum((a * b).reshape(8, 16, 128), axis=0))
-    st[...] = jnp.zeros((8, 128), F32)
-    for k in range(5):
-        rows = jnp.concatenate(sums[k], axis=0)
-        got = lax.dot_general(
-            ones, rows, (((1,), (1,)), ((), ())),
-            precision=lax.Precision.HIGHEST, preferred_element_type=F32,
-        )
-        st[k : k + 1, 0:48] = got[0:1, :]
+    local[6].wait()
+    forward(4)
+    plane_filter(3)
+    forward(1)
+    plane_filter(4)
+    mean_field(3)
+    (first_rim,) = own_plane([rim_product(window(4))])
+    z_m, z_r = own_plane(list(flat_mean(3)))
+    (second_t,) = own_span(3, [z_m], [z_r])
+    own_t, slopes_t = own_mean(3)
+    plane_filter(0)
+    forward(2)
+    mean_field(0)
+    component(0, first_rim, second_t, own_t, slopes_t)
+    for i in (1, 2):
+        plane_filter(i)
+        mean_field(i)
+        component(i, first_rim, second_t, own_t, slopes_t)
 
     group = xi * 2 + s
     st_a[group] = st[...]
@@ -389,10 +398,8 @@
     cells, clark, similar, sums, clark_out, similar_out, cc_out, sc_out,
     c_buf, s_buf, cc_buf, sc_buf, sem,
 ):
-    total = sums[:, 0:48] / cells
-    power_e, power_c, power_s = total[2:3], total[3:4], total[4:5]
-    clark_corr = total[0:1] / jnp.sqrt((power_e + small_eps) * (power_c + small_eps))
-    similar_corr = total[1:2] / jnp.sqrt((power_e + small_eps) * (power_s + small_eps))
+    total = sums[0:3, 0:80] / cells
+    power_e, power_c, power_s = total[:, 32:48], total[:, 48:64], total[:, 64:80]
     copies = []
 
     def send(src, dst):
@@ -400,24 +407,22 @@
         copy.start()
         copies.append(copy)
 
-    spot = lax.broadcasted_iota(jnp.int32, (48, 48), 0) == lax.broadcasted_iota(
-        jnp.int32, (48, 48), 1
+    spot = lax.broadcasted_iota(jnp.int32, (16, 16), 0) == lax.broadcasted_iota(
+        jnp.int32, (16, 16), 1
     )
     for power, values, buf, out in (
         (power_c, clark, c_buf, clark_out), (power_s, similar, s_buf, similar_out)
     ):
         scale = 1.0 / jnp.sqrt(power + small_eps)
-        scale = jnp.sum(
-            jnp.where(spot, jnp.broadcast_to(scale, (48, 48)), 0.0), axis=1, keepdims=True
-        )
         for i in range(3):
-            rows = jnp.broadcast_to(scale[16 * i : 16 * i + 16], (16, 128))
+            rows = jnp.where(spot, jnp.broadcast_to(scale[i : i + 1], (16, 16)), 0.0)
+            rows = jnp.broadcast_to(jnp.sum(rows, axis=1, keepdims=True), (16, 128))
             buf[i] = values[i] * rows[None]
             send(buf.at[i], out.at[i])
-    for corr, buf, out in ((clark_corr, cc_buf, cc_out), (similar_corr, sc_buf, sc_out)):
-        for i in range(3):
-            buf[i : i + 1, :] = corr[:, 16 * i : 16 * i + 16]
-        send(buf, out)
+    cc_buf[...] = total[:, 0:16] / jnp.sqrt((power_e + small_eps) * (power_c + small_eps))
+    send(cc_buf, cc_out)
+    sc_buf[...] = total[:, 16:32] / jnp.sqrt((power_e + small_eps) * (power_s + small_eps))
+    send(sc_buf, sc_out)
     for copy in copies:
         copy.wait()
 
@@ -450,7 +455,7 @@
             pltpu.VMEM((NQ, 512, 128), BF),
             pltpu.VMEM((NQ, 512, 128), BF),
             pltpu.VMEM((4, 18, 32, 128), F32),
-            pltpu.VMEM((16, 32, 128), F32),
+            pltpu.VMEM((4, 16, 32, 128), F32),
             pltpu.VMEM((8, 128), F32),
             pltpu.VMEM((2 * ROW, 8, 128), F32),
             pltpu.VMEM((8, 128), F32),

time: 45.5 us -> 42.2 us (0.927)
  the two profiles are of different devices: /device:TPU:25 before, /device:TPU:32 now
where the time goes in v3:
time: 42.2 us; the launch traced here: 42.1 us
  Pallas kernels  41.4 us (98%)
  between operations  0.64 us (2%)
    pallas_call x1, Pallas kernels, shards(): pl.pallas_call(kernel, out_shape=(flux, flux, jax.ShapeDtypeStruct((8, 12...  40.4 us
    pallas_call x1, Pallas kernels, shards(): pl.pallas_call(last, out_shape=(flux, flux, corr, corr), in_specs=[vmem]...  0.99 us

profile of v3, /device:TPU:32, one launch (start us, length us, event | category | flops | bytes accessed | tf_op | source)
XLA Modules:
  0.0 42.1 jit_solution(12854554311273721445)
XLA Ops:
  0.6 40.4 %shard_map.75 = (f32[3,8,16,128]{3,2,1,0:T(8,128)S(1)}, f32[3,8,16,128]{3,2,1,0:T(8,128)S(1)}, f32[8,128]{1,0:T(8,128)S(1)}) custom-call(f32[4,8,16,128]{3,2,1,0:T(8,128)} %fields.1, bf16[256,1536]{1,0:T(8,128)(2,1)} %constant.6.clone.km_in, bf16[2,128,1536]{2,1,0:T(8,128)(2,1)} %constant.7.clone.ko_in, bf16[4,768,256]{2,1,0:T(8,128)(2,1)} %constant.8.clone.w_in), custom_call_target="tpu_custom_call" | custom-call | flops 8000000000 | bytes 4000000 | tf_op jit(solution)/shard_map/pallas_call | solution.py:443
  41.1 1.0 %shard_map.76 = (f32[3,8,16,128]{3,2,1,0:T(8,128)}, f32[3,8,16,128]{3,2,1,0:T(8,128)}, f32[3,16]{1,0:T(4,128)}, f32[3,16]{1,0:T(4,128)}) custom-call(f32[3,8,16,128]{3,2,1,0:T(8,128)S(1)} %get-tuple-element.7.refs_0_, f32[3,8,16,128]{3,2,1,0:T(8,128)S(1)} %get-tuple-element.8.refs_1_, f32[8,128]{1,0:T(8,128)S(1)} %get-tuple-element.9.refs_2_), custom_call_target="tpu_custom_call" | custom-call | tf_op jit(solution)/shard_map/pallas_call | solution.py:482

commit v4 on v3

v4 whole, which is shorter than its diff:
```python
import math

import jax
import jax.numpy as jnp
import ml_dtypes
import numpy as np
from jax import lax
from jax.experimental import pallas as pl
from jax.experimental.pallas import tpu as pltpu
from jax.sharding import PartitionSpec as P

raw_taps = [math.exp(-((k - 8) ** 2) / 18.0) for k in range(17)]
filter_taps = [value / sum(raw_taps) for value in raw_taps]
clark_coef = 9.0
small_eps = 1e-06

MESH = pl.DeviceIdType.MESH
BF = jnp.bfloat16
F32 = jnp.float32
ROW = 4
NQ = 5


def tap(out_at, in_at):
    offset = in_at - out_at + 8
    inside = (offset >= 0) & (offset <= 16)
    return np.where(inside, np.array(filter_taps)[np.clip(offset, 0, 16)], 0.0)


def split(matrix):
    full = matrix.astype(np.float32)
    hi = full.astype(ml_dtypes.bfloat16)
    lo = (full - hi.astype(np.float32)).astype(ml_dtypes.bfloat16)
    return hi, lo


def left_stack(matrix):
    hi, lo = split(matrix)
    return np.concatenate([hi, hi, lo], axis=1)


def plane_matrices():
    near, w_out = np.meshgrid(np.arange(8), np.arange(16), indexing="ij")
    near, w_out = near.reshape(-1, 1), w_out.reshape(-1, 1)
    b, s, w = np.meshgrid(np.arange(2), np.arange(8), np.arange(16), indexing="ij")
    wall = tap(w_out + 8, (b * 16 + w).reshape(1, -1)) * 0.5
    direct, mirror = tap(near, s.reshape(1, -1)), tap(near, 15 - s.reshape(1, -1))
    folded = np.stack([left_stack((direct + mirror) * wall), left_stack((direct - mirror) * wall)])
    s_out, w_out = np.meshgrid(np.arange(16), np.arange(16), indexing="ij")
    s_out, w_out = s_out.reshape(-1, 1), w_out.reshape(-1, 1)
    s, w = np.meshgrid(np.arange(16), np.arange(32), indexing="ij")
    rows = tap(s_out, s.reshape(1, -1)) * tap(w_out + 8, w.reshape(1, -1))
    own = np.stack([left_stack(rows[:128]), left_stack(rows[128:])])
    return folded, own


def span_matrices():
    lane = np.arange(128)
    group, inner = lane // 32, lane % 32
    place = np.where(inner < 16, inner - 16, inner + 112)
    kept = (inner >= 8) & (inner < 24)
    result = []
    for f in range(4):
        columns = np.concatenate([lane, place])
        used = np.concatenate([lane >= 0, (group == f) & kept])
        cells = tap(columns[None, :], lane[:, None]) * used[None, :]
        rims = tap(columns[None, :], place[:32, None]) * used[None, :]
        (cell_hi, cell_lo), (rim_hi, rim_lo) = split(cells), split(rims)
        packed = np.zeros((128, 256), ml_dtypes.bfloat16)
        for k, part in enumerate((rim_hi, rim_hi, rim_lo)):
            at = 32 * ((f + k) % 4)
            packed[at : at + 32] = part
        result.append(np.concatenate([cell_hi, cell_hi, cell_lo, packed]))
    return np.stack(result)


def hi_lo(values):
    hi = values.astype(BF)
    return hi, (values - hi.astype(F32)).astype(BF)


def pack_rims(rims):
    hi = rims.astype(BF).astype(F32)
    group = lax.broadcasted_iota(jnp.int32, rims.shape, 1) // 32
    low, again = pltpu.roll(rims - hi, 32, 1), pltpu.roll(hi, 64, 1)

    def of_field(f):
        packed = jnp.where(group == f, hi, jnp.where(group == (f + 1) % 4, low, again))
        return packed.astype(BF)

    return of_field


def rim_product(rims):
    lane = lax.broadcasted_iota(jnp.int32, rims.shape, 1)
    last = jnp.where(lane >= 96, rims, 0.0)
    last = last + pltpu.roll(last, 32, 1)
    last = last + pltpu.roll(last, 64, 1)
    return rims * last


def kernel(
    fields, km_in, ko_in, w_in,
    clark_out, similar_out, sums_out,
    x, edge, edge_in, km, ko, wm, yh, yl, ys, m, mh, st, st_in,
    loc, z_s, z_r, y_s, y_r, e_s, e_r, a_s, a_r,
):
    p, wl, s = lax.axis_index("span"), lax.axis_index("wall"), lax.axis_index("stream")
    np_, nw = lax.axis_size("span"), lax.axis_size("wall")
    nz = np_ // ROW
    xi, zi = p % ROW, p // ROW
    o = 1 - s
    mine = pl.multiple_of(s * 8, 8)
    theirs = pl.multiple_of(o * 8, 8)

    mates = [
        {"span": ((zi + k // 8) % nz) * ROW + (xi + k % 8 // 2) % ROW, "stream": (s + k % 2) % 2}
        for k in sorted(range(1, 8 * nz), key=lambda k: -min(k // 8, nz - k // 8))
    ]
    ahead, behind = {"span": (p + 1) % np_}, {"span": (p + np_ - 1) % np_}
    above, below = {"wall": (wl + 1) % nw}, {"wall": (wl + nw - 1) % nw}
    greet = mates + [above, below]

    barrier = pltpu.get_barrier_semaphore()
    for device in greet:
        pl.semaphore_signal(barrier, inc=1, device_id=device, device_id_type=MESH)

    local = [
        pltpu.make_async_copy(fields, x.at[0:4, 1, pl.ds(mine, 8)], loc.at[0]),
        pltpu.make_async_copy(km_in, km, loc.at[1]),
        pltpu.make_async_copy(ko_in.at[s], ko, loc.at[2]),
        pltpu.make_async_copy(w_in, wm, loc.at[3]),
    ]
    for copy in local:
        copy.start()

    @pl.when(wl == 0)
    def _():
        x[:, 0] = jnp.zeros((NQ, 16, 16, 128), F32)

    @pl.when(wl == nw - 1)
    def _():
        x[:, 2] = jnp.zeros((NQ, 16, 16, 128), F32)

    local[0].wait()

    lane = lax.broadcasted_iota(jnp.int32, (64, 128), 1)
    to_next = jnp.zeros((64, 128), F32)
    to_prev = jnp.zeros((64, 128), F32)
    for f in range(4):
        for half in range(2):
            part = x[f, 1, pl.ds(mine, 8), 8 * half : 8 * half + 8, :].reshape(64, 128)
            at = f * 32 + 16 * half
            here = (lane >= at) & (lane < at + 16)
            to_next = jnp.where(here, pltpu.roll(part, (at - 112) % 128, 1), to_next)
            at = f * 32 + 16 * (1 - half)
            here = (lane >= at) & (lane < at + 16)
            to_prev = jnp.where(here, pltpu.roll(part, at % 128, 1) if at else part, to_prev)
    edge[0] = to_next.reshape(8, 8, 128)
    edge[1] = to_prev.reshape(8, 8, 128)

    pl.semaphore_wait(barrier, len(greet))

    def remote(src, dst, send, recv, device):
        return pltpu.make_async_remote_copy(
            src, dst, send, recv, device_id=device, device_id_type=MESH
        )

    def across(q):
        own = x.at[q, 1, pl.ds(mine, 8)]
        return remote(own, own, z_s.at[0], z_r.at[q], {"stream": o})

    def along(q, side, layers):
        return remote(
            x.at[q, 1, layers], x.at[q, 2 * side, layers],
            y_s.at[side], y_r.at[q, side], (above, below)[side],
        )

    def to_neighbours(q, layers):
        for side in range(2):

            @pl.when(wl < nw - 1 if side == 0 else wl > 0)
            def _(side=side):
                along(q, side, pl.ds(layers, 8)).start()

    def from_neighbours(q):
        for side in range(2):

            @pl.when(wl > 0 if side == 0 else wl < nw - 1)
            def _(side=side):
                along(q, side, pl.ds(0, 16)).wait_recv()

    def send_own(q):
        across(q).start()
        to_neighbours(q, mine)

    def forward(q):
        across(q).wait_recv()
        to_neighbours(q, theirs)

    def plane_filter(q):
        from_neighbours(q)
        folds = ([], [])
        for b in range(3):
            near = x[q, b, 0:8]
            far = jnp.concatenate([x[q, b, 15 - k : 16 - k] for k in range(8)], axis=0)
            folds[0].append(hi_lo((near + far).reshape(128, 128)))
            folds[1].append(hi_lo((near - far).reshape(128, 128)))

        def pair(blocks, k):
            return jnp.concatenate(
                [
                    jnp.concatenate([blocks[0][k], blocks[1][k]], axis=0),
                    jnp.concatenate([blocks[1][k], blocks[2][k]], axis=0),
                ],
                axis=1,
            )

        even, odd = [
            jnp.dot(
                km[k],
                jnp.concatenate([pair(fold, 0), pair(fold, 1), pair(fold, 0)], axis=0),
                preferred_element_type=F32,
            )
            for k, fold in enumerate(folds)
        ]
        near, far = even + odd, even - odd
        for half in range(2):
            lanes = slice(128 * half, 128 * half + 128)
            y = jnp.concatenate(
                [near[:, lanes]] + [far[112 - 16 * k : 128 - 16 * k, lanes] for k in range(8)],
                axis=0,
            )
            rows = slice(256 * half, 256 * half + 256)
            if q == 4:
                of_field = pack_rims(y)
                for f in range(4):
                    ys[f, rows, :] = of_field(f)
            else:
                yh[q, rows, :], yl[q, rows, :] = hi_lo(y)

    low = jnp.where(wl > 0, 1.0, 0.0)
    high = jnp.where(wl < nw - 1, 1.0, 0.0)

    def mean_field(f):
        out = jnp.dot(
            jnp.concatenate([yh[f], yl[f], yh[f], ys[f]], axis=1),
            wm[f],
            preferred_element_type=F32,
        ).reshape(2, 16, 16, 256)
        parts = (out[0, :, 0:8] * low, out[0, :, 8:16], out[1, :, 0:8], out[1, :, 8:16] * high)
        for k in range(4):
            m[f, 1:17, 8 * k : 8 * k + 8, :] = parts[k][:, :, :128]
            mh[f, :, 8 * k : 8 * k + 8, :] = parts[k][:, :, 128:]

    def window(q):
        return jnp.concatenate(
            [x[q, 0, :, 8:16, :], x[q, 1], x[q, 2, :, 0:8, :]], axis=1
        ).reshape(512, 128)

    def own_plane(values):
        hi, lo = hi_lo(jnp.concatenate(values, axis=1))
        out = jnp.dot(
            ko[...], jnp.concatenate([hi, lo, hi], axis=0), preferred_element_type=F32
        )
        return [out[:, 128 * k : 128 * k + 128] for k in range(len(values))]

    def own_span(f, bodies, rims):
        hi, lo = hi_lo(jnp.concatenate(bodies, axis=0))
        rim = jnp.concatenate([of_field(f) for of_field in rims], axis=0)
        out = jnp.dot(
            jnp.concatenate([hi, lo, hi, rim], axis=1),
            wm[f, :, 0:128],
            preferred_element_type=F32,
        )
        return [out[128 * k : 128 * k + 128] for k in range(len(bodies))]

    inner = pl.ds(1 + s * 8, 8)
    wide = lax.broadcasted_iota(jnp.int32, (128, 128), 1)

    def own_mean(f):
        c = m[f, inner, 8:24, :].reshape(128, 128)
        rim = mh[f, pl.ds(mine, 8), 8:24, :].reshape(128, 128)
        up = pltpu.roll(c, 127, 1)
        up = jnp.where(wide == 127, pltpu.roll(rim, (127 - (f * 32 + 16)) % 128, 1), up)
        down = pltpu.roll(c, 1, 1)
        down = jnp.where(wide == 0, pltpu.roll(rim, (128 - (f * 32 + 15)) % 128, 1), down)
        along_wall = m[f, inner, 9:25, :] - m[f, inner, 7:23, :]
        along_stream = m[f, pl.ds(2 + s * 8, 8), 8:24, :] - m[f, pl.ds(s * 8, 8), 8:24, :]
        return c, (
            (up - down) * 0.5,
            along_wall.reshape(128, 128) * 0.5,
            along_stream.reshape(128, 128) * 0.5,
        )

    def flat_mean(f):
        return m[f, 1:17].reshape(512, 128), mh[f].reshape(512, 128)

    ones = jnp.ones((8, 128), F32)

    def component(i, z_x, first_rim, second_t, own_t, slopes_t):
        mean, rim = flat_mean(i)
        mean_t, rim_t = flat_mean(3)
        shift = (32 * i - 96) % 128
        product_rim = rim * pltpu.roll(rim_t, shift, 1)
        both = rim + pltpu.roll(product_rim, (128 - shift) % 128, 1)
        parts = [mean, mean * mean_t, both]
        if z_x is None:
            z_m, z_p, z_r, z_x = own_plane(parts + [window(i) * window(3)])
        else:
            z_m, z_p, z_r = own_plane(parts)
        z_r = pack_rims(z_r)
        first, second = own_span(i, [z_x, z_m], [first_rim, z_r])
        (flux,) = own_span(3, [z_p], [z_r])
        own, slopes = own_mean(i)
        exact = first - own * own_t
        similar = flux - second * second_t
        total = slopes[0] * slopes_t[0] + slopes[1] * slopes_t[1]
        clark = clark_coef * (total + slopes[2] * slopes_t[2])
        clark_out[i] = clark.reshape(8, 16, 128)
        similar_out[i] = similar.reshape(8, 16, 128)
        pairs = (
            (exact, clark), (exact, similar), (exact, exact), (clark, clark), (similar, similar)
        )
        rows = [jnp.sum((a * b).reshape(8, 16, 128), axis=0) for a, b in pairs]
        got = lax.dot_general(
            ones, jnp.concatenate(rows, axis=0), (((1,), (1,)), ((), ())),
            precision=lax.Precision.HIGHEST, preferred_element_type=F32,
        )
        st[i : i + 1, 0:80] = got[0:1, :]

    across(3).start()
    for k, device in enumerate((ahead, behind)):
        remote(edge.at[k], edge_in.at[k], e_s.at[0], e_r.at[0], device).start()
    across(0).start()
    across(1).start()
    for q in (3, 0, 1):
        to_neighbours(q, mine)

    both_edges = remote(edge, edge_in, e_s.at[0], e_r.at[0], ahead)
    both_edges.wait_recv()
    before = edge_in[0].reshape(64, 128)
    after = edge_in[1].reshape(64, 128)
    left = lane % 32 < 16
    x[4, 1, pl.ds(mine, 8), 0:8, :] = jnp.where(left, before, after).reshape(8, 8, 128)
    x[4, 1, pl.ds(mine, 8), 8:16, :] = jnp.where(
        left, pltpu.roll(before, 112, 1), pltpu.roll(after, 16, 1)
    ).reshape(8, 8, 128)
    send_own(4)
    send_own(2)

    st[...] = jnp.zeros((8, 128), F32)
    m[:, 0] = jnp.zeros((4, 32, 128), F32)
    m[:, 17] = jnp.zeros((4, 32, 128), F32)
    forward(3)
    forward(0)
    for copy in local[1:]:
        copy.wait()
    forward(1)
    plane_filter(3)
    forward(4)
    plane_filter(0)
    forward(2)
    plane_filter(1)
    z_x = own_plane([window(i) * window(3) for i in range(2)])
    plane_filter(4)
    mean_field(3)
    first_rim, body_t, rim_t = own_plane([rim_product(window(4)), *flat_mean(3)])
    first_rim = pack_rims(first_rim)
    (second_t,) = own_span(3, [body_t], [pack_rims(rim_t)])
    own_t, slopes_t = own_mean(3)
    mean_field(0)
    component(0, z_x[0], first_rim, second_t, own_t, slopes_t)
    mean_field(1)
    component(1, z_x[1], first_rim, second_t, own_t, slopes_t)
    plane_filter(2)
    mean_field(2)
    component(2, None, first_rim, second_t, own_t, slopes_t)

    place = zi * 2 * ROW + xi * 2 + s
    st_in[place] = st[...]
    for device in mates:
        remote(st.at[0:3], st_in.at[place, 0:3], a_s.at[0], a_r.at[0], device).start()
    both_edges.wait_send()
    own = x.at[:, 1, pl.ds(mine, 8)]
    remote(own, own, z_s.at[0], z_r.at[0], {"stream": o}).wait_send()
    for side in range(2):

        @pl.when(wl < nw - 1 if side == 0 else wl > 0)
        def _(side=side):
            remote(
                x.at[:, 1], x.at[:, 2 * side], y_s.at[side], y_r.at[0, side], (above, below)[side]
            ).wait_send()

    several = st_in.at[0 : len(mates), 0:3]
    all_sums = remote(several, several, a_s.at[0], a_r.at[0], mates[0])
    all_sums.wait_recv()
    total = st_in[0, 0:3]
    for k in range(1, len(mates) + 1):
        total = total + st_in[k, 0:3]
    sums_out[0:3, :] = total
    sums_out[3:8, :] = jnp.zeros((5, 128), F32)

    all_sums.wait_send()


def finish(
    cells, clark, similar, sums, clark_out, similar_out, cc_out, sc_out,
    c_buf, s_buf, cc_buf, sc_buf, sem,
):
    total = sums[0:3, 0:80] / cells
    power_e, power_c, power_s = total[:, 32:48], total[:, 48:64], total[:, 64:80]
    copies = []

    def send(src, dst):
        copy = pltpu.make_async_copy(src, dst, sem.at[len(copies)])
        copy.start()
        copies.append(copy)

    spot = lax.broadcasted_iota(jnp.int32, (16, 16), 0) == lax.broadcasted_iota(
        jnp.int32, (16, 16), 1
    )
    for power, values, buf, out in (
        (power_c, clark, c_buf, clark_out), (power_s, similar, s_buf, similar_out)
    ):
        scale = 1.0 / jnp.sqrt(power + small_eps)
        for i in range(3):
            rows = jnp.where(spot, jnp.broadcast_to(scale[i : i + 1], (16, 16)), 0.0)
            rows = jnp.broadcast_to(jnp.sum(rows, axis=1, keepdims=True), (16, 128))
            buf[i] = values[i] * rows[None]
        send(buf, out)
    cc_buf[...] = total[:, 0:16] / jnp.sqrt((power_e + small_eps) * (power_c + small_eps))
    send(cc_buf, cc_out)
    sc_buf[...] = total[:, 16:32] / jnp.sqrt((power_e + small_eps) * (power_s + small_eps))
    send(sc_buf, sc_out)
    for copy in copies:
        copy.wait()


def shards(fields):
    nz = lax.axis_size("span") // ROW
    cells = float(
        fields.shape[1] * fields.shape[3] * lax.axis_size("stream") * lax.axis_size("span")
    )
    km, ko = plane_matrices()
    wm = span_matrices()
    vmem = pl.BlockSpec(memory_space=pltpu.VMEM)
    hbm = pl.BlockSpec(memory_space=pltpu.HBM)
    dma = pltpu.SemaphoreType.DMA

    flux = jax.ShapeDtypeStruct((3, 8, 16, 128), F32)
    corr = jax.ShapeDtypeStruct((3, 16), F32)
    clark, similar, sums = pl.pallas_call(
        kernel,
        out_shape=(flux, flux, jax.ShapeDtypeStruct((8, 128), F32)),
        in_specs=[hbm] * 4,
        out_specs=(vmem, vmem, vmem),
        scratch_shapes=[
            pltpu.VMEM((NQ, 3, 16, 16, 128), F32),
            pltpu.VMEM((2, 8, 8, 128), F32),
            pltpu.VMEM((2, 8, 8, 128), F32),
            pltpu.VMEM((2, 128, 768), BF),
            pltpu.VMEM((128, 1536), BF),
            pltpu.VMEM((4, 512, 256), BF),
            pltpu.VMEM((4, 512, 128), BF),
            pltpu.VMEM((4, 512, 128), BF),
            pltpu.VMEM((4, 512, 128), BF),
            pltpu.VMEM((4, 18, 32, 128), F32),
            pltpu.VMEM((4, 16, 32, 128), F32),
            pltpu.VMEM((8, 128), F32),
            pltpu.VMEM((2 * ROW * nz, 8, 128), F32),
            dma((4,)),
            dma((1,)), dma((NQ,)),
            dma((2,)), dma((NQ, 2)),
            dma((1,)), dma((1,)),
            dma((1,)), dma((1,)),
        ],
        compiler_params=pltpu.CompilerParams(
            collective_id=0, has_side_effects=True, vmem_limit_bytes=54680 * 2**10
        ),
        cost_estimate=pl.CostEstimate(
            flops=8_000_000_000, bytes_accessed=4_000_000, transcendentals=0
        ),
    )(fields, jnp.asarray(km), jnp.asarray(ko), jnp.asarray(wm))

    def last(*refs):
        finish(cells, *refs)

    return pl.pallas_call(
        last,
        out_shape=(flux, flux, corr, corr),
        in_specs=[vmem] * 3,
        out_specs=(hbm, hbm, hbm, hbm),
        scratch_shapes=[
            pltpu.VMEM((3, 8, 16, 128), F32),
            pltpu.VMEM((3, 8, 16, 128), F32),
            pltpu.VMEM((3, 16), F32),
            pltpu.VMEM((3, 16), F32),
            dma((4,)),
        ],
        compiler_params=pltpu.CompilerParams(vmem_limit_bytes=8 * 2**20),
    )(clark, similar, sums)


def solution(mesh):
    return jax.shard_map(
        shards,
        mesh=mesh,
        in_specs=(P(None, "stream", "wall", "span"),),
        out_specs=(
            P(None, "stream", "wall", "span"),
            P(None, "stream", "wall", "span"),
            P(None, "wall"),
            P(None, "wall"),
        ),
        check_vma=False,
    )
```

time: 42.2 us -> 40.1 us (0.950)
  Pallas kernels: 41.4 us -> 39.3 us
    pallas_call x1, Pallas kernels: 40.4 us -> 38.3 us  [shards(): pl.pallas_call(kernel, out_shape=(flux, flux, jax.ShapeDtypeStruct((8, 12...]
where the time goes in v4:
time: 40.1 us; the launch traced here: 39.9 us
  Pallas kernels  39.3 us (98%)
  between operations  0.64 us (2%)
    pallas_call x1, Pallas kernels, shards(): pl.pallas_call(kernel, out_shape=(flux, flux, jax.ShapeDtypeStruct((8, 12...  38.3 us
    pallas_call x1, Pallas kernels, shards(): pl.pallas_call(last, out_shape=(flux, flux, corr, corr), in_specs=[vmem]...  0.97 us

profile of v4, /device:TPU:32, one launch (start us, length us, event | category | flops | bytes accessed | tf_op | source)
XLA Modules:
  0.0 39.9 jit_solution(3818718056392196966)
XLA Ops:
  0.6 38.3 %shard_map.75 = (f32[3,8,16,128]{3,2,1,0:T(8,128)S(1)}, f32[3,8,16,128]{3,2,1,0:T(8,128)S(1)}, f32[8,128]{1,0:T(8,128)S(1)}) custom-call(f32[4,8,16,128]{3,2,1,0:T(8,128)} %fields.1, bf16[2,128,768]{2,1,0:T(8,128)(2,1)} %constant.6.clone.km_in, bf16[2,128,1536]{2,1,0:T(8,128)(2,1)} %constant.7.clone.ko_in, bf16[4,512,256]{2,1,0:T(8,128)(2,1)} %constant.8.clone.w_in), custom_call_target="tpu_custom_call" | custom-call | flops 8000000000 | bytes 4000000 | tf_op jit(solution)/shard_map/pallas_call | solution.py:453
  39.0 1.0 %shard_map.76 = (f32[3,8,16,128]{3,2,1,0:T(8,128)}, f32[3,8,16,128]{3,2,1,0:T(8,128)}, f32[3,16]{1,0:T(4,128)}, f32[3,16]{1,0:T(4,128)}) custom-call(f32[3,8,16,128]{3,2,1,0:T(8,128)S(1)} %get-tuple-element.7.refs_0_, f32[3,8,16,128]{3,2,1,0:T(8,128)S(1)} %get-tuple-element.8.refs_1_, f32[8,128]{1,0:T(8,128)S(1)} %get-tuple-element.9.refs_2_), custom_call_target="tpu_custom_call" | custom-call | tf_op jit(solution)/shard_map/pallas_call | solution.py:489

commit v5 on v4

--- a/solution.py
+++ b/solution.py
@@ -329,12 +329,11 @@
         )
         st[i : i + 1, 0:80] = got[0:1, :]
 
-    across(3).start()
     for k, device in enumerate((ahead, behind)):
         remote(edge.at[k], edge_in.at[k], e_s.at[0], e_r.at[0], device).start()
+    across(3).start()
     across(0).start()
-    across(1).start()
-    for q in (3, 0, 1):
+    for q in (3, 0):
         to_neighbours(q, mine)
 
     both_edges = remote(edge, edge_in, e_s.at[0], e_r.at[0], ahead)
@@ -346,8 +345,8 @@
     x[4, 1, pl.ds(mine, 8), 8:16, :] = jnp.where(
         left, pltpu.roll(before, 112, 1), pltpu.roll(after, 16, 1)
     ).reshape(8, 8, 128)
-    send_own(4)
-    send_own(2)
+    for q in (4, 1, 2):
+        send_own(q)
 
     st[...] = jnp.zeros((8, 128), F32)
     m[:, 0] = jnp.zeros((4, 32, 128), F32)
@@ -356,13 +355,12 @@
     forward(0)
     for copy in local[1:]:
         copy.wait()
+    forward(4)
+    plane_filter(3)
     forward(1)
-    plane_filter(3)
-    forward(4)
     plane_filter(0)
+    (z_x,) = own_plane([window(0) * window(3)])
     forward(2)
-    plane_filter(1)
-    z_x = own_plane([window(i) * window(3) for i in range(2)])
     plane_filter(4)
     mean_field(3)
     first_rim, body_t, rim_t = own_plane([rim_product(window(4)), *flat_mean(3)])
@@ -370,12 +368,11 @@
     (second_t,) = own_span(3, [body_t], [pack_rims(rim_t)])
     own_t, slopes_t = own_mean(3)
     mean_field(0)
-    component(0, z_x[0], first_rim, second_t, own_t, slopes_t)
-    mean_field(1)
-    component(1, z_x[1], first_rim, second_t, own_t, slopes_t)
-    plane_filter(2)
-    mean_field(2)
-    component(2, None, first_rim, second_t, own_t, slopes_t)
+    component(0, z_x, first_rim, second_t, own_t, slopes_t)
+    for i in (1, 2):
+        plane_filter(i)
+        mean_field(i)
+        component(i, None, first_rim, second_t, own_t, slopes_t)
 
     place = zi * 2 * ROW + xi * 2 + s
     st_in[place] = st[...]

time: 40.1 us -> 38.5 us (0.960)
  the two profiles are of different devices: /device:TPU:32 before, /device:TPU:25 now
where the time goes in v5:
time: 38.5 us; the launch traced here: 38.4 us
  Pallas kernels  37.8 us (98%)
  between operations  0.64 us (2%)
    pallas_call x1, Pallas kernels, shards(): pl.pallas_call(kernel, out_shape=(flux, flux, jax.ShapeDtypeStruct((8, 12...  36.8 us
    pallas_call x1, Pallas kernels, shards(): pl.pallas_call(last, out_shape=(flux, flux, corr, corr), in_specs=[vmem]...  0.97 us

profile of v5, /device:TPU:25, one launch (start us, length us, event | category | flops | bytes accessed | tf_op | source)
XLA Modules:
  0.0 38.4 jit_solution(11188538080801527802)
XLA Ops:
  0.6 36.8 %shard_map.75 = (f32[3,8,16,128]{3,2,1,0:T(8,128)S(1)}, f32[3,8,16,128]{3,2,1,0:T(8,128)S(1)}, f32[8,128]{1,0:T(8,128)S(1)}) custom-call(f32[4,8,16,128]{3,2,1,0:T(8,128)} %fields.1, bf16[2,128,768]{2,1,0:T(8,128)(2,1)} %constant.6.clone.km_in, bf16[2,128,1536]{2,1,0:T(8,128)(2,1)} %constant.7.clone.ko_in, bf16[4,512,256]{2,1,0:T(8,128)(2,1)} %constant.8.clone.w_in), custom_call_target="tpu_custom_call" | custom-call | flops 8000000000 | bytes 4000000 | tf_op jit(solution)/shard_map/pallas_call | solution.py:450
  37.4 1.0 %shard_map.76 = (f32[3,8,16,128]{3,2,1,0:T(8,128)}, f32[3,8,16,128]{3,2,1,0:T(8,128)}, f32[3,16]{1,0:T(4,128)}, f32[3,16]{1,0:T(4,128)}) custom-call(f32[3,8,16,128]{3,2,1,0:T(8,128)S(1)} %get-tuple-element.7.refs_0_, f32[3,8,16,128]{3,2,1,0:T(8,128)S(1)} %get-tuple-element.8.refs_1_, f32[8,128]{1,0:T(8,128)S(1)} %get-tuple-element.9.refs_2_), custom_call_target="tpu_custom_call" | custom-call | tf_op jit(solution)/shard_map/pallas_call | solution.py:486

commit v6 on v5

--- a/solution.py
+++ b/solution.py
@@ -177,7 +177,7 @@
         )
 
     def to_neighbours(q, layers):
-        for side in range(2):
+        for side in (1, 0):
 
             @pl.when(wl < nw - 1 if side == 0 else wl > 0)
             def _(side=side):
@@ -199,7 +199,6 @@
         to_neighbours(q, theirs)
 
     def plane_filter(q):
-        from_neighbours(q)
         folds = ([], [])
         for b in range(3):
             near = x[q, b, 0:8]
@@ -298,20 +297,18 @@
 
     ones = jnp.ones((8, 128), F32)
 
-    def component(i, z_x, first_rim, second_t, own_t, slopes_t):
+    def parts_of(i, place):
         mean, rim = flat_mean(i)
         mean_t, rim_t = flat_mean(3)
-        shift = (32 * i - 96) % 128
-        product_rim = rim * pltpu.roll(rim_t, shift, 1)
-        both = rim + pltpu.roll(product_rim, (128 - shift) % 128, 1)
-        parts = [mean, mean * mean_t, both]
-        if z_x is None:
-            z_m, z_p, z_r, z_x = own_plane(parts + [window(i) * window(3)])
-        else:
-            z_m, z_p, z_r = own_plane(parts)
+        product_rim = rim * pltpu.roll(rim_t, (32 * i - 96) % 128, 1)
+        both = rim + pltpu.roll(product_rim, 32 * (place - i) % 128, 1)
+        return [window(i) * window(3), mean, mean * mean_t, both]
+
+    def component(i, place, planes, first_rim, second_t, own_t, slopes_t):
+        z_x, z_m, z_p, z_r = planes
         z_r = pack_rims(z_r)
         first, second = own_span(i, [z_x, z_m], [first_rim, z_r])
-        (flux,) = own_span(3, [z_p], [z_r])
+        (flux,) = own_span(place, [z_p], [z_r])
         own, slopes = own_mean(i)
         exact = first - own * own_t
         similar = flux - second * second_t
@@ -356,23 +353,32 @@
     for copy in local[1:]:
         copy.wait()
     forward(4)
+    from_neighbours(3)
     plane_filter(3)
     forward(1)
+    from_neighbours(0)
     plane_filter(0)
-    (z_x,) = own_plane([window(0) * window(3)])
     forward(2)
+    from_neighbours(4)
     plane_filter(4)
     mean_field(3)
-    first_rim, body_t, rim_t = own_plane([rim_product(window(4)), *flat_mean(3)])
+    mean_field(0)
+    from_neighbours(1)
+    plane_filter(1)
+    parts = parts_of(0, 1)
+    mean_t, rim_t = flat_mean(3)
+    first_rim, z_t, *planes = own_plane(
+        [rim_product(window(4)), mean_t, *parts[:3], parts[3] + rim_t]
+    )
     first_rim = pack_rims(first_rim)
-    (second_t,) = own_span(3, [body_t], [pack_rims(rim_t)])
-    own_t, slopes_t = own_mean(3)
-    mean_field(0)
-    component(0, z_x, first_rim, second_t, own_t, slopes_t)
+    (second_t,) = own_span(3, [z_t], [pack_rims(planes[3])])
+    shared = (first_rim, second_t, *own_mean(3))
+    component(0, 1, planes, *shared)
+    from_neighbours(2)
+    plane_filter(2)
     for i in (1, 2):
-        plane_filter(i)
         mean_field(i)
-        component(i, None, first_rim, second_t, own_t, slopes_t)
+        component(i, 3, own_plane(parts_of(i, 3)), *shared)
 
     place = zi * 2 * ROW + xi * 2 + s
     st_in[place] = st[...]

time: 38.5 us -> 38.1 us (0.990)
  the two profiles are of different devices: /device:TPU:25 before, /device:TPU:32 now
where the time goes in v6:
time: 38.1 us; the launch traced here: 38 us
  Pallas kernels  37.3 us (98%)
  between operations  0.64 us (2%)
    pallas_call x1, Pallas kernels, shards(): pl.pallas_call(kernel, out_shape=(flux, flux, jax.ShapeDtypeStruct((8, 12...  36.4 us
    pallas_call x1, Pallas kernels, shards(): pl.pallas_call(last, out_shape=(flux, flux, corr, corr), in_specs=[vmem]...  0.97 us

profile of v6, /device:TPU:32, one launch (start us, length us, event | category | flops | bytes accessed | tf_op | source)
XLA Modules:
  0.0 38.0 jit_solution(11015879275167032987)
XLA Ops:
  0.6 36.4 %shard_map.75 = (f32[3,8,16,128]{3,2,1,0:T(8,128)S(1)}, f32[3,8,16,128]{3,2,1,0:T(8,128)S(1)}, f32[8,128]{1,0:T(8,128)S(1)}) custom-call(f32[4,8,16,128]{3,2,1,0:T(8,128)} %fields.1, bf16[2,128,768]{2,1,0:T(8,128)(2,1)} %constant.6.clone.km_in, bf16[2,128,1536]{2,1,0:T(8,128)(2,1)} %constant.7.clone.ko_in, bf16[4,512,256]{2,1,0:T(8,128)(2,1)} %constant.8.clone.w_in), custom_call_target="tpu_custom_call" | custom-call | flops 8000000000 | bytes 4000000 | tf_op jit(solution)/shard_map/pallas_call | solution.py:456
  37.0 1.0 %shard_map.76 = (f32[3,8,16,128]{3,2,1,0:T(8,128)}, f32[3,8,16,128]{3,2,1,0:T(8,128)}, f32[3,16]{1,0:T(4,128)}, f32[3,16]{1,0:T(4,128)}) custom-call(f32[3,8,16,128]{3,2,1,0:T(8,128)S(1)} %get-tuple-element.7.refs_0_, f32[3,8,16,128]{3,2,1,0:T(8,128)S(1)} %get-tuple-element.8.refs_1_, f32[8,128]{1,0:T(8,128)S(1)} %get-tuple-element.9.refs_2_), custom_call_target="tpu_custom_call" | custom-call | tf_op jit(solution)/shard_map/pallas_call | solution.py:492

commit v7 on v6

--- a/solution.py
+++ b/solution.py
@@ -295,7 +295,7 @@
     def flat_mean(f):
         return m[f, 1:17].reshape(512, 128), mh[f].reshape(512, 128)
 
-    ones = jnp.ones((8, 128), F32)
+    ones = jnp.ones((8, 384), BF)
 
     def parts_of(i, place):
         mean, rim = flat_mean(i)
@@ -320,9 +320,12 @@
             (exact, clark), (exact, similar), (exact, exact), (clark, clark), (similar, similar)
         )
         rows = [jnp.sum((a * b).reshape(8, 16, 128), axis=0) for a, b in pairs]
+        rows = jnp.concatenate(rows, axis=0)
+        high = rows.astype(BF)
+        middle, low = hi_lo(rows - high.astype(F32))
         got = lax.dot_general(
-            ones, jnp.concatenate(rows, axis=0), (((1,), (1,)), ((), ())),
-            precision=lax.Precision.HIGHEST, preferred_element_type=F32,
+            ones, jnp.concatenate([high, middle, low], axis=1), (((1,), (1,)), ((), ())),
+            preferred_element_type=F32,
         )
         st[i : i + 1, 0:80] = got[0:1, :]
 

time: 38.1 us -> 38.2 us (level)
  no operation moved by 1% of the time
where the time goes in v7:
time: 38.2 us; the launch traced here: 38.1 us
  Pallas kernels  37.4 us (98%)
  between operations  0.64 us (2%)
    pallas_call x1, Pallas kernels, shards(): pl.pallas_call(kernel, out_shape=(flux, flux, jax.ShapeDtypeStruct((8, 12...  36.5 us
    pallas_call x1, Pallas kernels, shards(): pl.pallas_call(last, out_shape=(flux, flux, corr, corr), in_specs=[vmem]...  0.97 us

profile of v7, /device:TPU:32, one launch (start us, length us, event | category | flops | bytes accessed | tf_op | source)
XLA Modules:
  0.0 38.1 jit_solution(15394960587394922345)
XLA Ops:
  0.6 36.5 %shard_map.75 = (f32[3,8,16,128]{3,2,1,0:T(8,128)S(1)}, f32[3,8,16,128]{3,2,1,0:T(8,128)S(1)}, f32[8,128]{1,0:T(8,128)S(1)}) custom-call(f32[4,8,16,128]{3,2,1,0:T(8,128)} %fields.1, bf16[2,128,768]{2,1,0:T(8,128)(2,1)} %constant.6.clone.km_in, bf16[2,128,1536]{2,1,0:T(8,128)(2,1)} %constant.7.clone.ko_in, bf16[4,512,256]{2,1,0:T(8,128)(2,1)} %constant.8.clone.w_in), custom_call_target="tpu_custom_call" | custom-call | flops 8000000000 | bytes 4000000 | tf_op jit(solution)/shard_map/pallas_call | solution.py:459
  37.1 1.0 %shard_map.76 = (f32[3,8,16,128]{3,2,1,0:T(8,128)}, f32[3,8,16,128]{3,2,1,0:T(8,128)}, f32[3,16]{1,0:T(4,128)}, f32[3,16]{1,0:T(4,128)}) custom-call(f32[3,8,16,128]{3,2,1,0:T(8,128)S(1)} %get-tuple-element.7.refs_0_, f32[3,8,16,128]{3,2,1,0:T(8,128)S(1)} %get-tuple-element.8.refs_1_, f32[8,128]{1,0:T(8,128)S(1)} %get-tuple-element.9.refs_2_), custom_call_target="tpu_custom_call" | custom-call | tf_op jit(solution)/shard_map/pallas_call | solution.py:495

commit v8 on v6

--- a/solution.py
+++ b/solution.py
@@ -166,9 +166,9 @@
             src, dst, send, recv, device_id=device, device_id_type=MESH
         )
 
-    def across(q):
-        own = x.at[q, 1, pl.ds(mine, 8)]
-        return remote(own, own, z_s.at[0], z_r.at[q], {"stream": o})
+    def across(q, half):
+        own = x.at[q, 1, pl.ds(mine + 4 * half, 4)]
+        return remote(own, own, z_s.at[0], z_r.at[q, half], {"stream": o})
 
     def along(q, side, layers):
         return remote(
@@ -176,12 +176,12 @@
             y_s.at[side], y_r.at[q, side], (above, below)[side],
         )
 
-    def to_neighbours(q, layers):
+    def to_neighbours(q, start, count):
         for side in (1, 0):
 
             @pl.when(wl < nw - 1 if side == 0 else wl > 0)
             def _(side=side):
-                along(q, side, pl.ds(layers, 8)).start()
+                along(q, side, pl.ds(start, count)).start()
 
     def from_neighbours(q):
         for side in range(2):
@@ -191,12 +191,14 @@
                 along(q, side, pl.ds(0, 16)).wait_recv()
 
     def send_own(q):
-        across(q).start()
-        to_neighbours(q, mine)
+        for half in range(2):
+            across(q, half).start()
+        to_neighbours(q, mine, 8)
 
     def forward(q):
-        across(q).wait_recv()
-        to_neighbours(q, theirs)
+        for half in range(2):
+            across(q, half).wait_recv()
+            to_neighbours(q, theirs + 4 * half, 4)
 
     def plane_filter(q):
         folds = ([], [])
@@ -328,10 +330,11 @@
 
     for k, device in enumerate((ahead, behind)):
         remote(edge.at[k], edge_in.at[k], e_s.at[0], e_r.at[0], device).start()
-    across(3).start()
-    across(0).start()
     for q in (3, 0):
-        to_neighbours(q, mine)
+        for half in range(2):
+            across(q, half).start()
+    for q in (3, 0):
+        to_neighbours(q, mine, 8)
 
     both_edges = remote(edge, edge_in, e_s.at[0], e_r.at[0], ahead)
     both_edges.wait_recv()
@@ -386,7 +389,7 @@
         remote(st.at[0:3], st_in.at[place, 0:3], a_s.at[0], a_r.at[0], device).start()
     both_edges.wait_send()
     own = x.at[:, 1, pl.ds(mine, 8)]
-    remote(own, own, z_s.at[0], z_r.at[0], {"stream": o}).wait_send()
+    remote(own, own, z_s.at[0], z_r.at[0, 0], {"stream": o}).wait_send()
     for side in range(2):
 
         @pl.when(wl < nw - 1 if side == 0 else wl > 0)
@@ -473,7 +476,7 @@
             pltpu.VMEM((8, 128), F32),
             pltpu.VMEM((2 * ROW * nz, 8, 128), F32),
             dma((4,)),
-            dma((1,)), dma((NQ,)),
+            dma((1,)), dma((NQ, 2)),
             dma((2,)), dma((NQ, 2)),
             dma((1,)), dma((1,)),
             dma((1,)), dma((1,)),

time: 38.1 us -> 38.2 us (level)
  no operation moved by 1% of the time
where the time goes in v8:
time: 38.2 us; the launch traced here: 38 us
  Pallas kernels  37.4 us (98%)
  between operations  0.64 us (2%)
    pallas_call x1, Pallas kernels, shards(): pl.pallas_call(kernel, out_shape=(flux, flux, jax.ShapeDtypeStruct((8, 12...  36.4 us
    pallas_call x1, Pallas kernels, shards(): pl.pallas_call(last, out_shape=(flux, flux, corr, corr), in_specs=[vmem]...  0.97 us

profile of v8, /device:TPU:32, one launch (start us, length us, event | category | flops | bytes accessed | tf_op | source)
XLA Modules:
  0.0 38.0 jit_solution(12520652442937440020)
XLA Ops:
  0.6 36.4 %shard_map.75 = (f32[3,8,16,128]{3,2,1,0:T(8,128)S(1)}, f32[3,8,16,128]{3,2,1,0:T(8,128)S(1)}, f32[8,128]{1,0:T(8,128)S(1)}) custom-call(f32[4,8,16,128]{3,2,1,0:T(8,128)} %fields.1, bf16[2,128,768]{2,1,0:T(8,128)(2,1)} %constant.6.clone.km_in, bf16[2,128,1536]{2,1,0:T(8,128)(2,1)} %constant.7.clone.ko_in, bf16[4,512,256]{2,1,0:T(8,128)(2,1)} %constant.8.clone.w_in), custom_call_target="tpu_custom_call" | custom-call | flops 8000000000 | bytes 4000000 | tf_op jit(solution)/shard_map/pallas_call | solution.py:459
  37.0 1.0 %shard_map.76 = (f32[3,8,16,128]{3,2,1,0:T(8,128)}, f32[3,8,16,128]{3,2,1,0:T(8,128)}, f32[3,16]{1,0:T(4,128)}, f32[3,16]{1,0:T(4,128)}) custom-call(f32[3,8,16,128]{3,2,1,0:T(8,128)S(1)} %get-tuple-element.7.refs_0_, f32[3,8,16,128]{3,2,1,0:T(8,128)S(1)} %get-tuple-element.8.refs_1_, f32[8,128]{1,0:T(8,128)S(1)} %get-tuple-element.9.refs_2_), custom_call_target="tpu_custom_call" | custom-call | tf_op jit(solution)/shard_map/pallas_call | solution.py:495
